TPU v7x, 32 devices: a whole 2x2x4 slice. The times are simulated.
32 devices in a mesh: groups: 2 (over y), slabx: 4 (over z), slaby: 2 (over x), section: 2 (over core).
Axes of the slice: x: 2, y: 2, z: 4, core: 2. Of those that a mesh axis runs over, the one named last changes fastest.
Arguments:
- nodes: bfloat16 [4, 6144, 512], P(None, ('groups', 'slabx', 'slaby')), parts along dimension 1, may hold values from -6 to 6
- tile_index: int32 [48, 4], P(('groups', 'slabx', 'slaby')), parts along dimension 0, may hold values from 0 to 6, as said below
- tile_values: bfloat16 [48, 4, 128, 128], P(('groups', 'slabx', 'slaby')), parts along dimension 0, may hold values from -0.25 to 0.25
- halo_rows: int32 [16, 4, 128], P(('groups', 'slabx', 'slaby')), parts along dimension 0, may hold values from 0 to 383, as said below
- w_msg: bfloat16 [2, 512, 512], P('section'), may hold values from -0.25 to 0.25
- w_in: bfloat16 [2, 1024, 512], P('section'), may hold values from -0.1875 to 0.1875
- w_out: bfloat16 [2, 512, 512], P('section'), may hold values from -0.25 to 0.25
- bias: float32 [2, 512], P('section'), may hold values from -3 to 3
- gain: float32 [2, 512], P('section'), may hold values from 0.1 to 1.9
Outputs:
- updated: bfloat16 [4, 6144, 512], P('section', ('groups', 'slabx', 'slaby')), parts along dimension 1
There are 2 independent parts, one for each index of `groups`. A program takes and returns all parts, laid end to end along the dimension named above; an argument that names none is the same for every part. Nothing has to cross between parts.
Inputs may be any that keep to these rules, and one draw needn't show every extreme that they name: `tile_index`: row tile r of a slab lists itself first, then one tile of its own slab, then two of the halo tiles 3 .. 6; all four halo tiles appear in every slab's lists. `halo_rows`: each list holds 128 distinct local rows of its slab, among them row 0 and row 383.
All inputs are finite; a program needn't handle non-finite values.
Results may differ from a plain program's by a relative error of at most 0.013.
Values may be sent and summed in bfloat16 or wider, within the bound.
No kernel may reach another device: no remote copies, remote signals or barrier semaphores. Data moves between devices by JAX's collectives and lax.ppermute only.
A program may use at most 64 MiB of HBM per device.

v0:
```python
import jax
import jax.numpy as jnp
from jax import lax
from jax.sharding import PartitionSpec as P


def shifted(block, axis, distance):
    devices = range(lax.axis_size(axis))
    route = [(i - distance, i) for i in devices if i - distance in devices]
    return lax.ppermute(block, axis, route)


def layer_step(
    state, tile_index, tile_values, halo_rows, weight_msg, weight_in, weight_out, bias_row, gain_row
):
    batch, rows, width = state.shape
    tile = tile_values.shape[-1]
    tiles = rows // tile
    msg = jnp.einsum("bnd,de->bne", state, weight_msg, preferred_element_type=jnp.float32).astype(
        jnp.bfloat16
    )
    picked = jnp.take(msg, halo_rows[0], axis=1)
    from_lower_x = shifted(picked[:, 0], "slabx", 1)
    from_upper_x = shifted(picked[:, 1], "slabx", -1)
    from_lower_y = shifted(picked[:, 2], "slaby", 1)
    from_upper_y = shifted(picked[:, 3], "slaby", -1)
    arrived = jnp.stack([from_lower_x, from_upper_x, from_lower_y, from_upper_y], axis=1)
    extended = jnp.concatenate([msg.reshape(batch, tiles, tile, width), arrived], axis=1)
    gathered = jnp.take(extended, tile_index, axis=1)
    agg = jnp.einsum("rkij,brkjd->brid", tile_values, gathered, preferred_element_type=jnp.float32)
    agg = agg.astype(jnp.bfloat16).reshape(batch, rows, width)
    joined = jnp.concatenate([state, agg], axis=-1)
    pre = (
        jnp.einsum("bnc,ce->bne", joined, weight_in, preferred_element_type=jnp.float32) + bias_row
    )
    act = jnp.maximum(pre, 0.0).astype(jnp.bfloat16)
    out = jnp.einsum("bnc,ce->bne", act, weight_out, preferred_element_type=jnp.float32)
    mean = jnp.mean(out, axis=-1, keepdims=True)
    var = jnp.mean(jnp.square(out - mean), axis=-1, keepdims=True)
    normed = (out - mean) / jnp.sqrt(var + 1e-05)
    return (state.astype(jnp.float32) + gain_row * normed).astype(jnp.bfloat16)


def shards(nodes, tile_index, tile_values, halo_rows, w_msg, w_in, w_out, bias, gain):
    snaps = nodes.shape[0]
    half = snaps // 2
    section_id = lax.axis_index("section")

    def one_tick(received, tick):
        fresh = lax.dynamic_index_in_dim(nodes, jnp.minimum(tick, snaps - 1), 0, keepdims=True)
        current = jnp.where(section_id == 0, fresh, received)
        result = layer_step(
            current,
            tile_index,
            tile_values,
            halo_rows,
            w_msg[0],
            w_in[0],
            w_out[0],
            bias[0],
            gain[0],
        )
        passed = shifted(result, "section", 1)
        return (passed, result[0])

    start = jnp.zeros((1,) + nodes.shape[1:], jnp.bfloat16)
    _, results = lax.scan(one_tick, start, jnp.arange(snaps + 1, dtype=jnp.int32))
    finals = results[1:]
    returned = shifted(finals[:half], "section", -1)
    return jnp.where(section_id == 0, returned, finals[half:])


def solution(mesh):
    in_specs = (
        P(None, ("groups", "slabx", "slaby"), None),
        P(("groups", "slabx", "slaby"), None),
        P(("groups", "slabx", "slaby"), None, None, None),
        P(("groups", "slabx", "slaby"), None, None),
        P("section", None, None),
        P("section", None, None),
        P("section", None, None),
        P("section", None),
        P("section", None),
    )
    out_specs = P("section", ("groups", "slabx", "slaby"), None)
    return jax.shard_map(shards, mesh=mesh, in_specs=in_specs, out_specs=out_specs, check_vma=False)
```

profile of v0, /device:TPU:0, one launch (start us, length us, event | category | flops | bytes accessed | tf_op | source)
XLA Modules:
  0.0 157.0 jit_solution(16285776024761565753)
XLA Ops:
  0.0 149.5 %while.14 = (s32[]{:T(128)}, bf16[1,384,512]{2,1,0:T(8,128)(2,1)S(1)}, bf16[5,384,512]{2,1,0:T(8,128)(2,1)}, pred[]{:T(512)}, s32[5]{0:T(128)S(1)}, /*index=5*/b...) while((s32[]{:T(128)}, ...), condition=%wide.region_3.4_spmd, body=%wide.region_0.3_spmd.sunk | while | flops 1012407296 | bytes 24172612 | solution.py:67
  5.1 2.0 %gather_fusion = bf16[512,512]{1,0:T(8,128)(2,1)S(1)} fusion(bf16[384,512]{1,0:T(8,128)(2,1)S(1)} %convolution_convert_fusion.2, s32[1024]{0:T(1024)S(1)} %pad_clamp_fusion.4), kind=kCustom, calls=%fused_computation.clone.1 | custom fusion | bytes 1050624 | tf_op jit(solution)/shard_map/while/body/eval_jaxpr/jit(_take)/gather | solution.py:22
  7.3 5.0 %collective-permute-start = (bf16[1,128,512]{2,1,0:T(8,128)(2,1)S(1)}, bf16[1,128,512]{2,1,0:T(8,128)(2,1)S(1)}, u32[]{:S(2)}, u32[]{:S(2)}) collective-permute-start(bf16[1,128,512]{2,1,0:T(8,128)(2,1)S(1)} %get-tuple-element.295), channel_id=1, source_target_pairs={{0,4},{4,8},{8,12},{1,5},{5,9},{9,13},{2,6},{6,10},{10,14},{3,7},{... | collective-permute-start | bytes 393224 | tf_op jit(solution)/shard_map/while/body/eval_jaxpr/ppermute | solution.py:10
  13.6 3.4 %collective-permute-start.2 = (bf16[1,128,512]{2,1,0:T(8,128)(2,1)S(1)}, bf16[1,128,512]{2,1,0:T(8,128)(2,1)S(1)}, u32[]{:S(2)}, u32[]{:S(2)}) collective-permute-start(bf16[1,128,512]{2,1,0:T(8,128)(2,1)S(1)} %get-tuple-element.297), channel_id=1, source_target_pairs={{0,2},{1,3},{4,6},{5,7},{8,10},{9,11},{12,14},{13,15},{16,18},{17,... | collective-permute-start | bytes 393224 | tf_op jit(solution)/shard_map/while/body/eval_jaxpr/ppermute | solution.py:10
  19.5 4.4 %collective-permute-done.3 = bf16[1,128,512]{2,1,0:T(8,128)(2,1)S(1)} collective-permute-done((bf16[1,128,512]{2,1,0:T(8,128)(2,1)S(1)}, bf16[1,128,512]{2,1,0:T(8,128)(2,1)S(1)}, u32[]{:S(2)}, u32[]{:S(2)}) %collective-permute-start.3) | collective-permute-done | bytes 131104 | tf_op jit(solution)/shard_map/while/body/eval_jaxpr/ppermute | solution.py:10
  25.5 2.3 %fusion.50 = (f32[384]{0:T(512)S(1)}, f32[384,512]{1,0:T(8,128)S(1)}) fusion(bf16[1,512,512]{2,1,0:T(8,128)(2,1)} %get-tuple-element.352, bf16[1,1024,512]{2,1,0:T(8,128)(2,1)} %get-tuple-element.350, bf16[1,384,512]{2,1,0:T(8,128)(2,1)S(1)} %bitcast.128, bf16[1,384,512]{2,1,0:T(8,128)(2,1)S(1)} %dynamic-slice_select_fusion.2, f32[512]{0:T(512)S(1)} %bitcast.127), kind=kOutput, calls=%fused_computation.52.clone.1 | convolution fusion | flops 606338688 | bytes 3149312 | tf_op jit(solution)/shard_map/while/body/eval_jaxpr/bnc,ce->bne/dot_general | solution.py:37
  36.8 2.0 %gather_fusion = bf16[512,512]{1,0:T(8,128)(2,1)S(1)} fusion(bf16[384,512]{1,0:T(8,128)(2,1)S(1)} %convolution_convert_fusion.2, s32[1024]{0:T(1024)S(1)} %pad_clamp_fusion.4), kind=kCustom, calls=%fused_computation.clone.1 | custom fusion | bytes 1050624 | tf_op jit(solution)/shard_map/while/body/eval_jaxpr/jit(_take)/gather | solution.py:22
  38.9 4.6 %collective-permute-start = (bf16[1,128,512]{2,1,0:T(8,128)(2,1)S(1)}, bf16[1,128,512]{2,1,0:T(8,128)(2,1)S(1)}, u32[]{:S(2)}, u32[]{:S(2)}) collective-permute-start(bf16[1,128,512]{2,1,0:T(8,128)(2,1)S(1)} %get-tuple-element.295), channel_id=1, source_target_pairs={{0,4},{4,8},{8,12},{1,5},{5,9},{9,13},{2,6},{6,10},{10,14},{3,7},{... | collective-permute-start | bytes 393224 | tf_op jit(solution)/shard_map/while/body/eval_jaxpr/ppermute | solution.py:10
  44.8 1.5 collective-permute-start.2
  47.8 3.1 %collective-permute-done.1 = bf16[1,128,512]{2,1,0:T(8,128)(2,1)S(1)} collective-permute-done((bf16[1,128,512]{2,1,0:T(8,128)(2,1)S(1)}, bf16[1,128,512]{2,1,0:T(8,128)(2,1)S(1)}, u32[]{:S(2)}, u32[]{:S(2)}) %collective-permute-start.1) | collective-permute-done | bytes 131104 | tf_op jit(solution)/shard_map/while/body/eval_jaxpr/ppermute | solution.py:10
  50.9 2.6 %collective-permute-done.3 = bf16[1,128,512]{2,1,0:T(8,128)(2,1)S(1)} collective-permute-done((bf16[1,128,512]{2,1,0:T(8,128)(2,1)S(1)}, bf16[1,128,512]{2,1,0:T(8,128)(2,1)S(1)}, u32[]{:S(2)}, u32[]{:S(2)}) %collective-permute-start.3) | collective-permute-done | bytes 131104 | tf_op jit(solution)/shard_map/while/body/eval_jaxpr/ppermute | solution.py:10
  55.2 2.3 %fusion.50 = (f32[384]{0:T(512)S(1)}, f32[384,512]{1,0:T(8,128)S(1)}) fusion(bf16[1,512,512]{2,1,0:T(8,128)(2,1)} %get-tuple-element.352, bf16[1,1024,512]{2,1,0:T(8,128)(2,1)} %get-tuple-element.350, bf16[1,384,512]{2,1,0:T(8,128)(2,1)S(1)} %bitcast.128, bf16[1,384,512]{2,1,0:T(8,128)(2,1)S(1)} %dynamic-slice_select_fusion.2, f32[512]{0:T(512)S(1)} %bitcast.127), kind=kOutput, calls=%fused_computation.52.clone.1 | convolution fusion | flops 606338688 | bytes 3149312 | tf_op jit(solution)/shard_map/while/body/eval_jaxpr/bnc,ce->bne/dot_general | solution.py:37
  66.4 2.0 %gather_fusion = bf16[512,512]{1,0:T(8,128)(2,1)S(1)} fusion(bf16[384,512]{1,0:T(8,128)(2,1)S(1)} %convolution_convert_fusion.2, s32[1024]{0:T(1024)S(1)} %pad_clamp_fusion.4), kind=kCustom, calls=%fused_computation.clone.1 | custom fusion | bytes 1050624 | tf_op jit(solution)/shard_map/while/body/eval_jaxpr/jit(_take)/gather | solution.py:22
  68.6 4.3 %collective-permute-start = (bf16[1,128,512]{2,1,0:T(8,128)(2,1)S(1)}, bf16[1,128,512]{2,1,0:T(8,128)(2,1)S(1)}, u32[]{:S(2)}, u32[]{:S(2)}) collective-permute-start(bf16[1,128,512]{2,1,0:T(8,128)(2,1)S(1)} %get-tuple-element.295), channel_id=1, source_target_pairs={{0,4},{4,8},{8,12},{1,5},{5,9},{9,13},{2,6},{6,10},{10,14},{3,7},{... | collective-permute-start | bytes 393224 | tf_op jit(solution)/shard_map/while/body/eval_jaxpr/ppermute | solution.py:10
  74.2 1.5 collective-permute-start.2
  77.1 3.1 %collective-permute-done.1 = bf16[1,128,512]{2,1,0:T(8,128)(2,1)S(1)} collective-permute-done((bf16[1,128,512]{2,1,0:T(8,128)(2,1)S(1)}, bf16[1,128,512]{2,1,0:T(8,128)(2,1)S(1)}, u32[]{:S(2)}, u32[]{:S(2)}) %collective-permute-start.1) | collective-permute-done | bytes 131104 | tf_op jit(solution)/shard_map/while/body/eval_jaxpr/ppermute | solution.py:10
  80.3 2.6 %collective-permute-done.3 = bf16[1,128,512]{2,1,0:T(8,128)(2,1)S(1)} collective-permute-done((bf16[1,128,512]{2,1,0:T(8,128)(2,1)S(1)}, bf16[1,128,512]{2,1,0:T(8,128)(2,1)S(1)}, u32[]{:S(2)}, u32[]{:S(2)}) %collective-permute-start.3) | collective-permute-done | bytes 131104 | tf_op jit(solution)/shard_map/while/body/eval_jaxpr/ppermute | solution.py:10
  84.6 2.3 %fusion.50 = (f32[384]{0:T(512)S(1)}, f32[384,512]{1,0:T(8,128)S(1)}) fusion(bf16[1,512,512]{2,1,0:T(8,128)(2,1)} %get-tuple-element.352, bf16[1,1024,512]{2,1,0:T(8,128)(2,1)} %get-tuple-element.350, bf16[1,384,512]{2,1,0:T(8,128)(2,1)S(1)} %bitcast.128, bf16[1,384,512]{2,1,0:T(8,128)(2,1)S(1)} %dynamic-slice_select_fusion.2, f32[512]{0:T(512)S(1)} %bitcast.127), kind=kOutput, calls=%fused_computation.52.clone.1 | convolution fusion | flops 606338688 | bytes 3149312 | tf_op jit(solution)/shard_map/while/body/eval_jaxpr/bnc,ce->bne/dot_general | solution.py:37
  95.8 2.0 %gather_fusion = bf16[512,512]{1,0:T(8,128)(2,1)S(1)} fusion(bf16[384,512]{1,0:T(8,128)(2,1)S(1)} %convolution_convert_fusion.2, s32[1024]{0:T(1024)S(1)} %pad_clamp_fusion.4), kind=kCustom, calls=%fused_computation.clone.1 | custom fusion | bytes 1050624 | tf_op jit(solution)/shard_map/while/body/eval_jaxpr/jit(_take)/gather | solution.py:22
  98.0 4.3 %collective-permute-start = (bf16[1,128,512]{2,1,0:T(8,128)(2,1)S(1)}, bf16[1,128,512]{2,1,0:T(8,128)(2,1)S(1)}, u32[]{:S(2)}, u32[]{:S(2)}) collective-permute-start(bf16[1,128,512]{2,1,0:T(8,128)(2,1)S(1)} %get-tuple-element.295), channel_id=1, source_target_pairs={{0,4},{4,8},{8,12},{1,5},{5,9},{9,13},{2,6},{6,10},{10,14},{3,7},{... | collective-permute-start | bytes 393224 | tf_op jit(solution)/shard_map/while/body/eval_jaxpr/ppermute | solution.py:10
  103.6 1.5 collective-permute-start.2
  106.5 3.1 %collective-permute-done.1 = bf16[1,128,512]{2,1,0:T(8,128)(2,1)S(1)} collective-permute-done((bf16[1,128,512]{2,1,0:T(8,128)(2,1)S(1)}, bf16[1,128,512]{2,1,0:T(8,128)(2,1)S(1)}, u32[]{:S(2)}, u32[]{:S(2)}) %collective-permute-start.1) | collective-permute-done | bytes 131104 | tf_op jit(solution)/shard_map/while/body/eval_jaxpr/ppermute | solution.py:10
  109.7 2.6 %collective-permute-done.3 = bf16[1,128,512]{2,1,0:T(8,128)(2,1)S(1)} collective-permute-done((bf16[1,128,512]{2,1,0:T(8,128)(2,1)S(1)}, bf16[1,128,512]{2,1,0:T(8,128)(2,1)S(1)}, u32[]{:S(2)}, u32[]{:S(2)}) %collective-permute-start.3) | collective-permute-done | bytes 131104 | tf_op jit(solution)/shard_map/while/body/eval_jaxpr/ppermute | solution.py:10
  114.0 2.3 %fusion.50 = (f32[384]{0:T(512)S(1)}, f32[384,512]{1,0:T(8,128)S(1)}) fusion(bf16[1,512,512]{2,1,0:T(8,128)(2,1)} %get-tuple-element.352, bf16[1,1024,512]{2,1,0:T(8,128)(2,1)} %get-tuple-element.350, bf16[1,384,512]{2,1,0:T(8,128)(2,1)S(1)} %bitcast.128, bf16[1,384,512]{2,1,0:T(8,128)(2,1)S(1)} %dynamic-slice_select_fusion.2, f32[512]{0:T(512)S(1)} %bitcast.127), kind=kOutput, calls=%fused_computation.52.clone.1 | convolution fusion | flops 606338688 | bytes 3149312 | tf_op jit(solution)/shard_map/while/body/eval_jaxpr/bnc,ce->bne/dot_general | solution.py:37
  125.2 2.0 %gather_fusion = bf16[512,512]{1,0:T(8,128)(2,1)S(1)} fusion(bf16[384,512]{1,0:T(8,128)(2,1)S(1)} %convolution_convert_fusion.2, s32[1024]{0:T(1024)S(1)} %pad_clamp_fusion.4), kind=kCustom, calls=%fused_computation.clone.1 | custom fusion | bytes 1050624 | tf_op jit(solution)/shard_map/while/body/eval_jaxpr/jit(_take)/gather | solution.py:22
  127.4 4.3 %collective-permute-start = (bf16[1,128,512]{2,1,0:T(8,128)(2,1)S(1)}, bf16[1,128,512]{2,1,0:T(8,128)(2,1)S(1)}, u32[]{:S(2)}, u32[]{:S(2)}) collective-permute-start(bf16[1,128,512]{2,1,0:T(8,128)(2,1)S(1)} %get-tuple-element.295), channel_id=1, source_target_pairs={{0,4},{4,8},{8,12},{1,5},{5,9},{9,13},{2,6},{6,10},{10,14},{3,7},{... | collective-permute-start | bytes 393224 | tf_op jit(solution)/shard_map/while/body/eval_jaxpr/ppermute | solution.py:10
  133.0 1.5 collective-permute-start.2
  135.9 3.1 %collective-permute-done.1 = bf16[1,128,512]{2,1,0:T(8,128)(2,1)S(1)} collective-permute-done((bf16[1,128,512]{2,1,0:T(8,128)(2,1)S(1)}, bf16[1,128,512]{2,1,0:T(8,128)(2,1)S(1)}, u32[]{:S(2)}, u32[]{:S(2)}) %collective-permute-start.1) | collective-permute-done | bytes 131104 | tf_op jit(solution)/shard_map/while/body/eval_jaxpr/ppermute | solution.py:10
  139.1 2.6 %collective-permute-done.3 = bf16[1,128,512]{2,1,0:T(8,128)(2,1)S(1)} collective-permute-done((bf16[1,128,512]{2,1,0:T(8,128)(2,1)S(1)}, bf16[1,128,512]{2,1,0:T(8,128)(2,1)S(1)}, u32[]{:S(2)}, u32[]{:S(2)}) %collective-permute-start.3) | collective-permute-done | bytes 131104 | tf_op jit(solution)/shard_map/while/body/eval_jaxpr/ppermute | solution.py:10
  143.3 2.3 %fusion.50 = (f32[384]{0:T(512)S(1)}, f32[384,512]{1,0:T(8,128)S(1)}) fusion(bf16[1,512,512]{2,1,0:T(8,128)(2,1)} %get-tuple-element.352, bf16[1,1024,512]{2,1,0:T(8,128)(2,1)} %get-tuple-element.350, bf16[1,384,512]{2,1,0:T(8,128)(2,1)S(1)} %bitcast.128, bf16[1,384,512]{2,1,0:T(8,128)(2,1)S(1)} %dynamic-slice_select_fusion.2, f32[512]{0:T(512)S(1)} %bitcast.127), kind=kOutput, calls=%fused_computation.52.clone.1 | convolution fusion | flops 606338688 | bytes 3149312 | tf_op jit(solution)/shard_map/while/body/eval_jaxpr/bnc,ce->bne/dot_general | solution.py:37
  152.0 2.9 %collective-permute-done.5 = bf16[2,384,512]{2,1,0:T(8,128)(2,1)S(1)} collective-permute-done((bf16[2,384,512]{2,1,0:T(8,128)(2,1)S(1)}, bf16[2,384,512]{2,1,0:T(8,128)(2,1)S(1)}, u32[]{:S(2)}, u32[]{:S(2)}) %collective-permute-start.5) | collective-permute-done | bytes 786464 | tf_op jit(solution)/shard_map/ppermute | solution.py:10
  154.9 2.1 %slice_select_fusion = bf16[2,384,512]{2,1,0:T(8,128)(2,1)} fusion(bf16[2,384,512]{2,1,0:T(8,128)(2,1)S(1)} %collective-permute-done.5, bf16[5,384,512]{2,1,0:T(8,128)(2,1)} %get-tuple-element.165, pred[]{:T(512)} %eq.6), kind=kLoop, calls=%fused_computation.51 | loop fusion | flops 393216 | bytes 2359297 | tf_op jit(solution)/shard_map/jit(_where)/select_n | solution.py:70
  (191 shorter events, 67.9 us)
Async XLA Ops:
  7.1 11.2 %copy-start = (s32[3,4]{1,0:T(4,128)S(1)}, s32[3,4]{1,0:T(4,128)}, u32[]{:S(2)}) copy-start(s32[3,4]{1,0:T(4,128)} %get-tuple-element.346) | copy-start | bytes 148 | tf_op jit(solution)/shard_map/while
  7.3 11.1 %collective-permute-start = (bf16[1,128,512]{2,1,0:T(8,128)(2,1)S(1)}, bf16[1,128,512]{2,1,0:T(8,128)(2,1)S(1)}, u32[]{:S(2)}, u32[]{:S(2)}) collective-permute-start(bf16[1,128,512]{2,1,0:T(8,128)(2,1)S(1)} %get-tuple-element.295), channel_id=1, source_target_pairs={{0,4},{4,8},{8,12},{1,5},{5,9},{9,13},{2,6},{6,10},{10,14},{3,7},{... | collective-permute-start | bytes 393224 | tf_op jit(solution)/shard_map/while/body/eval_jaxpr/ppermute | solution.py:10
  12.3 6.9 %collective-permute-start.1 = (bf16[1,128,512]{2,1,0:T(8,128)(2,1)S(1)}, bf16[1,128,512]{2,1,0:T(8,128)(2,1)S(1)}, u32[]{:S(2)}, u32[]{:S(2)}) collective-permute-start(bf16[1,128,512]{2,1,0:T(8,128)(2,1)S(1)} %get-tuple-element.296), channel_id=1, source_target_pairs={{4,0},{8,4},{12,8},{5,1},{9,5},{13,9},{6,2},{10,6},{14,10},{7,3},{... | collective-permute-start | bytes 393224 | tf_op jit(solution)/shard_map/while/body/eval_jaxpr/ppermute | solution.py:10
  13.6 5.9 %collective-permute-start.2 = (bf16[1,128,512]{2,1,0:T(8,128)(2,1)S(1)}, bf16[1,128,512]{2,1,0:T(8,128)(2,1)S(1)}, u32[]{:S(2)}, u32[]{:S(2)}) collective-permute-start(bf16[1,128,512]{2,1,0:T(8,128)(2,1)S(1)} %get-tuple-element.297), channel_id=1, source_target_pairs={{0,2},{1,3},{4,6},{5,7},{8,10},{9,11},{12,14},{13,15},{16,18},{17,... | collective-permute-start | bytes 393224 | tf_op jit(solution)/shard_map/while/body/eval_jaxpr/ppermute | solution.py:10
  17.0 6.9 %collective-permute-start.3 = (bf16[1,128,512]{2,1,0:T(8,128)(2,1)S(1)}, bf16[1,128,512]{2,1,0:T(8,128)(2,1)S(1)}, u32[]{:S(2)}, u32[]{:S(2)}) collective-permute-start(bf16[1,128,512]{2,1,0:T(8,128)(2,1)S(1)} %get-tuple-element.298), channel_id=1, source_target_pairs={{2,0},{3,1},{6,4},{7,5},{10,8},{11,9},{14,12},{15,13},{18,16},{19,... | collective-permute-start | bytes 393224 | tf_op jit(solution)/shard_map/while/body/eval_jaxpr/ppermute | solution.py:10
  25.5 2.5 %copy-start.1 = (f32[1,512]{1,0:T(1,128)S(1)}, f32[1,512]{1,0:T(1,128)}, u32[]{:S(2)}) copy-start(f32[1,512]{1,0:T(1,128)} %get-tuple-element.345) | copy-start | bytes 6148 | tf_op jit(solution)/shard_map/while
  29.1 2.6 %collective-permute-start.4 = (bf16[1,384,512]{2,1,0:T(8,128)(2,1)S(1)}, bf16[1,384,512]{2,1,0:T(8,128)(2,1)S(1)}, u32[]{:S(2)}, u32[]{:S(2)}) collective-permute-start(bf16[1,384,512]{2,1,0:T(8,128)(2,1)S(1)} %get-tuple-element.301), channel_id=1, source_target_pairs={{0,1},{2,3},{4,5},{6,7},{8,9},{10,11},{12,13},{14,15},{16,17},{18,... | collective-permute-start | bytes 1179656 | tf_op jit(solution)/shard_map/while/body/eval_jaxpr/ppermute | solution.py:10
  38.7 8.9 %copy-start = (s32[3,4]{1,0:T(4,128)S(1)}, s32[3,4]{1,0:T(4,128)}, u32[]{:S(2)}) copy-start(s32[3,4]{1,0:T(4,128)} %get-tuple-element.346) | copy-start | bytes 148 | tf_op jit(solution)/shard_map/while
  38.9 8.8 %collective-permute-start = (bf16[1,128,512]{2,1,0:T(8,128)(2,1)S(1)}, bf16[1,128,512]{2,1,0:T(8,128)(2,1)S(1)}, u32[]{:S(2)}, u32[]{:S(2)}) collective-permute-start(bf16[1,128,512]{2,1,0:T(8,128)(2,1)S(1)} %get-tuple-element.295), channel_id=1, source_target_pairs={{0,4},{4,8},{8,12},{1,5},{5,9},{9,13},{2,6},{6,10},{10,14},{3,7},{... | collective-permute-start | bytes 393224 | tf_op jit(solution)/shard_map/while/body/eval_jaxpr/ppermute | solution.py:10
  43.5 7.4 %collective-permute-start.1 = (bf16[1,128,512]{2,1,0:T(8,128)(2,1)S(1)}, bf16[1,128,512]{2,1,0:T(8,128)(2,1)S(1)}, u32[]{:S(2)}, u32[]{:S(2)}) collective-permute-start(bf16[1,128,512]{2,1,0:T(8,128)(2,1)S(1)} %get-tuple-element.296), channel_id=1, source_target_pairs={{4,0},{8,4},{12,8},{5,1},{9,5},{13,9},{6,2},{10,6},{14,10},{7,3},{... | collective-permute-start | bytes 393224 | tf_op jit(solution)/shard_map/while/body/eval_jaxpr/ppermute | solution.py:10
  44.8 6.1 %collective-permute-start.2 = (bf16[1,128,512]{2,1,0:T(8,128)(2,1)S(1)}, bf16[1,128,512]{2,1,0:T(8,128)(2,1)S(1)}, u32[]{:S(2)}, u32[]{:S(2)}) collective-permute-start(bf16[1,128,512]{2,1,0:T(8,128)(2,1)S(1)} %get-tuple-element.297), channel_id=1, source_target_pairs={{0,2},{1,3},{4,6},{5,7},{8,10},{9,11},{12,14},{13,15},{16,18},{17,... | collective-permute-start | bytes 393224 | tf_op jit(solution)/shard_map/while/body/eval_jaxpr/ppermute | solution.py:10
  46.3 7.2 %collective-permute-start.3 = (bf16[1,128,512]{2,1,0:T(8,128)(2,1)S(1)}, bf16[1,128,512]{2,1,0:T(8,128)(2,1)S(1)}, u32[]{:S(2)}, u32[]{:S(2)}) collective-permute-start(bf16[1,128,512]{2,1,0:T(8,128)(2,1)S(1)} %get-tuple-element.298), channel_id=1, source_target_pairs={{2,0},{3,1},{6,4},{7,5},{10,8},{11,9},{14,12},{15,13},{18,16},{19,... | collective-permute-start | bytes 393224 | tf_op jit(solution)/shard_map/while/body/eval_jaxpr/ppermute | solution.py:10
  58.7 2.6 %collective-permute-start.4 = (bf16[1,384,512]{2,1,0:T(8,128)(2,1)S(1)}, bf16[1,384,512]{2,1,0:T(8,128)(2,1)S(1)}, u32[]{:S(2)}, u32[]{:S(2)}) collective-permute-start(bf16[1,384,512]{2,1,0:T(8,128)(2,1)S(1)} %get-tuple-element.301), channel_id=1, source_target_pairs={{0,1},{2,3},{4,5},{6,7},{8,9},{10,11},{12,13},{14,15},{16,17},{18,... | collective-permute-start | bytes 1179656 | tf_op jit(solution)/shard_map/while/body/eval_jaxpr/ppermute | solution.py:10
  68.4 8.6 %copy-start = (s32[3,4]{1,0:T(4,128)S(1)}, s32[3,4]{1,0:T(4,128)}, u32[]{:S(2)}) copy-start(s32[3,4]{1,0:T(4,128)} %get-tuple-element.346) | copy-start | bytes 148 | tf_op jit(solution)/shard_map/while
  68.6 8.5 %collective-permute-start = (bf16[1,128,512]{2,1,0:T(8,128)(2,1)S(1)}, bf16[1,128,512]{2,1,0:T(8,128)(2,1)S(1)}, u32[]{:S(2)}, u32[]{:S(2)}) collective-permute-start(bf16[1,128,512]{2,1,0:T(8,128)(2,1)S(1)} %get-tuple-element.295), channel_id=1, source_target_pairs={{0,4},{4,8},{8,12},{1,5},{5,9},{9,13},{2,6},{6,10},{10,14},{3,7},{... | collective-permute-start | bytes 393224 | tf_op jit(solution)/shard_map/while/body/eval_jaxpr/ppermute | solution.py:10
  72.9 7.4 %collective-permute-start.1 = (bf16[1,128,512]{2,1,0:T(8,128)(2,1)S(1)}, bf16[1,128,512]{2,1,0:T(8,128)(2,1)S(1)}, u32[]{:S(2)}, u32[]{:S(2)}) collective-permute-start(bf16[1,128,512]{2,1,0:T(8,128)(2,1)S(1)} %get-tuple-element.296), channel_id=1, source_target_pairs={{4,0},{8,4},{12,8},{5,1},{9,5},{13,9},{6,2},{10,6},{14,10},{7,3},{... | collective-permute-start | bytes 393224 | tf_op jit(solution)/shard_map/while/body/eval_jaxpr/ppermute | solution.py:10
  74.2 6.1 %collective-permute-start.2 = (bf16[1,128,512]{2,1,0:T(8,128)(2,1)S(1)}, bf16[1,128,512]{2,1,0:T(8,128)(2,1)S(1)}, u32[]{:S(2)}, u32[]{:S(2)}) collective-permute-start(bf16[1,128,512]{2,1,0:T(8,128)(2,1)S(1)} %get-tuple-element.297), channel_id=1, source_target_pairs={{0,2},{1,3},{4,6},{5,7},{8,10},{9,11},{12,14},{13,15},{16,18},{17,... | collective-permute-start | bytes 393224 | tf_op jit(solution)/shard_map/while/body/eval_jaxpr/ppermute | solution.py:10
  75.6 7.2 %collective-permute-start.3 = (bf16[1,128,512]{2,1,0:T(8,128)(2,1)S(1)}, bf16[1,128,512]{2,1,0:T(8,128)(2,1)S(1)}, u32[]{:S(2)}, u32[]{:S(2)}) collective-permute-start(bf16[1,128,512]{2,1,0:T(8,128)(2,1)S(1)} %get-tuple-element.298), channel_id=1, source_target_pairs={{2,0},{3,1},{6,4},{7,5},{10,8},{11,9},{14,12},{15,13},{18,16},{19,... | collective-permute-start | bytes 393224 | tf_op jit(solution)/shard_map/while/body/eval_jaxpr/ppermute | solution.py:10
  88.1 2.6 %collective-permute-start.4 = (bf16[1,384,512]{2,1,0:T(8,128)(2,1)S(1)}, bf16[1,384,512]{2,1,0:T(8,128)(2,1)S(1)}, u32[]{:S(2)}, u32[]{:S(2)}) collective-permute-start(bf16[1,384,512]{2,1,0:T(8,128)(2,1)S(1)} %get-tuple-element.301), channel_id=1, source_target_pairs={{0,1},{2,3},{4,5},{6,7},{8,9},{10,11},{12,13},{14,15},{16,17},{18,... | collective-permute-start | bytes 1179656 | tf_op jit(solution)/shard_map/while/body/eval_jaxpr/ppermute | solution.py:10
  97.8 8.5 %copy-start = (s32[3,4]{1,0:T(4,128)S(1)}, s32[3,4]{1,0:T(4,128)}, u32[]{:S(2)}) copy-start(s32[3,4]{1,0:T(4,128)} %get-tuple-element.346) | copy-start | bytes 148 | tf_op jit(solution)/shard_map/while
  98.0 8.5 %collective-permute-start = (bf16[1,128,512]{2,1,0:T(8,128)(2,1)S(1)}, bf16[1,128,512]{2,1,0:T(8,128)(2,1)S(1)}, u32[]{:S(2)}, u32[]{:S(2)}) collective-permute-start(bf16[1,128,512]{2,1,0:T(8,128)(2,1)S(1)} %get-tuple-element.295), channel_id=1, source_target_pairs={{0,4},{4,8},{8,12},{1,5},{5,9},{9,13},{2,6},{6,10},{10,14},{3,7},{... | collective-permute-start | bytes 393224 | tf_op jit(solution)/shard_map/while/body/eval_jaxpr/ppermute | solution.py:10
  102.3 7.4 %collective-permute-start.1 = (bf16[1,128,512]{2,1,0:T(8,128)(2,1)S(1)}, bf16[1,128,512]{2,1,0:T(8,128)(2,1)S(1)}, u32[]{:S(2)}, u32[]{:S(2)}) collective-permute-start(bf16[1,128,512]{2,1,0:T(8,128)(2,1)S(1)} %get-tuple-element.296), channel_id=1, source_target_pairs={{4,0},{8,4},{12,8},{5,1},{9,5},{13,9},{6,2},{10,6},{14,10},{7,3},{... | collective-permute-start | bytes 393224 | tf_op jit(solution)/shard_map/while/body/eval_jaxpr/ppermute | solution.py:10
  103.6 6.1 %collective-permute-start.2 = (bf16[1,128,512]{2,1,0:T(8,128)(2,1)S(1)}, bf16[1,128,512]{2,1,0:T(8,128)(2,1)S(1)}, u32[]{:S(2)}, u32[]{:S(2)}) collective-permute-start(bf16[1,128,512]{2,1,0:T(8,128)(2,1)S(1)} %get-tuple-element.297), channel_id=1, source_target_pairs={{0,2},{1,3},{4,6},{5,7},{8,10},{9,11},{12,14},{13,15},{16,18},{17,... | collective-permute-start | bytes 393224 | tf_op jit(solution)/shard_map/while/body/eval_jaxpr/ppermute | solution.py:10
  105.0 7.2 %collective-permute-start.3 = (bf16[1,128,512]{2,1,0:T(8,128)(2,1)S(1)}, bf16[1,128,512]{2,1,0:T(8,128)(2,1)S(1)}, u32[]{:S(2)}, u32[]{:S(2)}) collective-permute-start(bf16[1,128,512]{2,1,0:T(8,128)(2,1)S(1)} %get-tuple-element.298), channel_id=1, source_target_pairs={{2,0},{3,1},{6,4},{7,5},{10,8},{11,9},{14,12},{15,13},{18,16},{19,... | collective-permute-start | bytes 393224 | tf_op jit(solution)/shard_map/while/body/eval_jaxpr/ppermute | solution.py:10
  117.5 2.6 %collective-permute-start.4 = (bf16[1,384,512]{2,1,0:T(8,128)(2,1)S(1)}, bf16[1,384,512]{2,1,0:T(8,128)(2,1)S(1)}, u32[]{:S(2)}, u32[]{:S(2)}) collective-permute-start(bf16[1,384,512]{2,1,0:T(8,128)(2,1)S(1)} %get-tuple-element.301), channel_id=1, source_target_pairs={{0,1},{2,3},{4,5},{6,7},{8,9},{10,11},{12,13},{14,15},{16,17},{18,... | collective-permute-start | bytes 1179656 | tf_op jit(solution)/shard_map/while/body/eval_jaxpr/ppermute | solution.py:10
  127.2 8.5 %copy-start = (s32[3,4]{1,0:T(4,128)S(1)}, s32[3,4]{1,0:T(4,128)}, u32[]{:S(2)}) copy-start(s32[3,4]{1,0:T(4,128)} %get-tuple-element.346) | copy-start | bytes 148 | tf_op jit(solution)/shard_map/while
  127.4 8.5 %collective-permute-start = (bf16[1,128,512]{2,1,0:T(8,128)(2,1)S(1)}, bf16[1,128,512]{2,1,0:T(8,128)(2,1)S(1)}, u32[]{:S(2)}, u32[]{:S(2)}) collective-permute-start(bf16[1,128,512]{2,1,0:T(8,128)(2,1)S(1)} %get-tuple-element.295), channel_id=1, source_target_pairs={{0,4},{4,8},{8,12},{1,5},{5,9},{9,13},{2,6},{6,10},{10,14},{3,7},{... | collective-permute-start | bytes 393224 | tf_op jit(solution)/shard_map/while/body/eval_jaxpr/ppermute | solution.py:10
  131.7 7.4 %collective-permute-start.1 = (bf16[1,128,512]{2,1,0:T(8,128)(2,1)S(1)}, bf16[1,128,512]{2,1,0:T(8,128)(2,1)S(1)}, u32[]{:S(2)}, u32[]{:S(2)}) collective-permute-start(bf16[1,128,512]{2,1,0:T(8,128)(2,1)S(1)} %get-tuple-element.296), channel_id=1, source_target_pairs={{4,0},{8,4},{12,8},{5,1},{9,5},{13,9},{6,2},{10,6},{14,10},{7,3},{... | collective-permute-start | bytes 393224 | tf_op jit(solution)/shard_map/while/body/eval_jaxpr/ppermute | solution.py:10
  133.0 6.1 %collective-permute-start.2 = (bf16[1,128,512]{2,1,0:T(8,128)(2,1)S(1)}, bf16[1,128,512]{2,1,0:T(8,128)(2,1)S(1)}, u32[]{:S(2)}, u32[]{:S(2)}) collective-permute-start(bf16[1,128,512]{2,1,0:T(8,128)(2,1)S(1)} %get-tuple-element.297), channel_id=1, source_target_pairs={{0,2},{1,3},{4,6},{5,7},{8,10},{9,11},{12,14},{13,15},{16,18},{17,... | collective-permute-start | bytes 393224 | tf_op jit(solution)/shard_map/while/body/eval_jaxpr/ppermute | solution.py:10
  134.4 7.2 %collective-permute-start.3 = (bf16[1,128,512]{2,1,0:T(8,128)(2,1)S(1)}, bf16[1,128,512]{2,1,0:T(8,128)(2,1)S(1)}, u32[]{:S(2)}, u32[]{:S(2)}) collective-permute-start(bf16[1,128,512]{2,1,0:T(8,128)(2,1)S(1)} %get-tuple-element.298), channel_id=1, source_target_pairs={{2,0},{3,1},{6,4},{7,5},{10,8},{11,9},{14,12},{15,13},{18,16},{19,... | collective-permute-start | bytes 393224 | tf_op jit(solution)/shard_map/while/body/eval_jaxpr/ppermute | solution.py:10
  146.9 2.6 %collective-permute-start.4 = (bf16[1,384,512]{2,1,0:T(8,128)(2,1)S(1)}, bf16[1,384,512]{2,1,0:T(8,128)(2,1)S(1)}, u32[]{:S(2)}, u32[]{:S(2)}) collective-permute-start(bf16[1,384,512]{2,1,0:T(8,128)(2,1)S(1)} %get-tuple-element.301), channel_id=1, source_target_pairs={{0,1},{2,3},{4,5},{6,7},{8,9},{10,11},{12,13},{14,15},{16,17},{18,... | collective-permute-start | bytes 1179656 | tf_op jit(solution)/shard_map/while/body/eval_jaxpr/ppermute | solution.py:10
  150.7 4.2 %collective-permute-start.5 = (bf16[2,384,512]{2,1,0:T(8,128)(2,1)S(1)}, bf16[2,384,512]{2,1,0:T(8,128)(2,1)S(1)}, u32[]{:S(2)}, u32[]{:S(2)}) collective-permute-start(bf16[2,384,512]{2,1,0:T(8,128)(2,1)S(1)} %slice.29), channel_id=1, source_target_pairs={{1,0},{3,2},{5,4},{7,6},{9,8},{11,10},{13,12},{15,14},{17,16},{19,... | collective-permute-start | bytes 2359304 | tf_op jit(solution)/shard_map/ppermute | solution.py:10
  (14 other events, 18.6 us)
where the time goes:
time: 159 us; the launch traced here: 157 us
  starting transfers between devices  52.3 us (33%)
  waiting for transfers between devices  37.5 us (24%)
  other arithmetic  21.2 us (13%)
  matrix products  21.1 us (13%)
  local copies, waits for them, and re-layouts  20.6 us (13%)
  loops' own time  4.18 us (3%)
    ppermute x26, starting transfers between devices, shifted(): return lax.ppermute(block, axis, route)  52.3 us
    ppermute x26, waiting for transfers between devices, shifted(): return lax.ppermute(block, axis, route)  37.5 us
    dot_general x5, matrix products, layer_step(): jnp.einsum('bnc,ce->bne', act, weight_out, preferred_element_type=jnp.flo...  11.4 us
    gather x5, local copies, waits for them, and re-layouts, layer_step(): picked = jnp.take(msg, halo_rows[0], axis=1)  9.86 us
    dot_general x5, matrix products, layer_step(): jnp.einsum('bnd,de->bne', state, weight_msg, preferred_element_type=jnp.f...  7.03 us
    select_n x5, other arithmetic, one_tick(): current = jnp.where(section_id == 0, fresh, received)  5.22 us
    dynamic_update_slice x5, other arithmetic, shards(): lax.scan(one_tick, start, jnp.arange(snaps + 1, dtype=jnp.int32))  4.95 us
    another operation x1, loops' own time, shards(): lax.scan(one_tick, start, jnp.arange(snaps + 1, dtype=jnp.int32))  4.18 us
  transfers between devices with their start and end apart: 26, of which 17 were waited for; matrix products, arithmetic and copies ran while one was open for 1% of the time, Pallas kernels for 0%

commit v1 on v0

v1 whole, which is shorter than its diff:
```python
import functools

import jax
import jax.numpy as jnp
from jax import lax
from jax.experimental import pallas as pl
from jax.experimental.pallas import tpu as pltpu
from jax.sharding import PartitionSpec as P

F32 = jnp.float32
BF16 = jnp.bfloat16
LIMIT = 24 * 1024 * 1024
AXES = ("slabx", "slaby")


def dot(a, b):
    return jnp.dot(a, b, preferred_element_type=F32)


def meetings(sizes):
    return [(axis, turn) for axis in range(2) for turn in range(2) if sizes[axis] > 1 + turn]


def swap(block, axis, turn):
    size = lax.axis_size(AXES[axis])
    route = []
    for low in range(turn, size - 1, 2):
        route += [(low, low + 1), (low + 1, low)]
    return lax.ppermute(block, AXES[axis], route)


def select_rows(halo_ref, rounds, rows):
    picks = []
    for axis, turn in rounds:
        odd = lax.rem(lax.axis_index(AXES[axis]), 2)
        which = 2 * axis + (odd if turn == 0 else 1 - odd)
        listed = halo_ref[0, pl.ds(which, 1), :]
        count = listed.shape[1]
        down = jnp.transpose(jnp.broadcast_to(listed, (count, count)))
        for at in range(0, rows, count):
            columns = lax.broadcasted_iota(jnp.int32, (count, count), 1) + at
            picks.append((down == columns).astype(F32).astype(BF16))
    per = rows // count
    return jnp.concatenate(
        [
            jnp.concatenate(picks[n * per : (n + 1) * per], axis=1)
            for n in range(len(rounds))
        ],
        axis=0,
    )


def pick_kernel(rounds, halo_ref, nodes_ref, state_ref, *rest):
    sends, (sem,) = rest[: len(rounds)], rest[len(rounds) :]
    half, rows, _ = state_ref.shape
    section = lax.axis_index("section")
    fetch = [
        pltpu.make_async_copy(nodes_ref.at[section * half + b], state_ref.at[b], sem.at[b])
        for b in range(half)
    ]
    for copy in fetch:
        copy.start()
    chosen = select_rows(halo_ref, rounds, rows)
    count = chosen.shape[0] // len(rounds)
    for b in range(half):
        fetch[b].wait()
        sent = dot(chosen, state_ref[b]).astype(BF16)
        for n, ref in enumerate(sends):
            ref[b] = sent[n * count : (n + 1) * count]


def local_work(index_ref, values_ref, state, w_in, w_msg, bias, half, base_ref, near_ref, fold_ref):
    tiles, _, tile, _ = values_ref.shape
    width = w_msg.shape[0]
    top, bottom = w_in[:width], w_in[width:]
    fold_ref[...] = dot(w_msg, bottom).astype(BF16)
    for b in range(half):
        base_ref[b] = dot(state[b], top) + bias
        for r in range(tiles):
            other = pl.multiple_of(index_ref[r, 1] * tile, tile)
            pair = jnp.concatenate(
                [state[b, r * tile : (r + 1) * tile, :], state[b, pl.ds(other, tile), :]], axis=0
            )
            edges = jnp.concatenate([values_ref[r, 0], values_ref[r, 1]], axis=1)
            near_ref[b, r * tile : (r + 1) * tile, :] = dot(edges, pair)


def local_kernel(
    layer, index_ref, values_ref, state_ref,
    msg_a, msg_b, in_a, in_b, out_a, out_b, vec_a, vec_b,
    base_ref, near_ref, fold_ref, last_ref, gain_ref,
):
    mine = lax.axis_index("section") == layer
    half = base_ref.shape[0]
    pick = lambda a, b: jnp.where(mine, a[...], b[...])
    vec = pick(vec_a, vec_b)
    gain_ref[...] = vec[1:2]
    last_ref[...] = pick(out_a, out_b)[0]
    local_work(
        index_ref, values_ref, state_ref, pick(in_a, in_b)[0], pick(msg_a, msg_b)[0], vec[0:1],
        half, base_ref, near_ref, fold_ref,
    )


def finish_kernel(
    rounds, final, index_ref, values_ref, halo_ref, state_ref,
    base_ref, near_ref, fold_ref, last_ref, gain_ref, *rest,
):
    recvs, rest = rest[: len(rounds)], rest[len(rounds) :]
    out_ref, rest = rest[0], rest[1:]
    sends, rest = ((), rest) if final else (rest[: len(rounds)], rest[len(rounds) :])
    ext = rest[0]
    half, rows, width = base_ref.shape
    tiles, _, tile, _ = values_ref.shape
    for slot in range(4):
        here = (slot // 2, slot % 2)
        if here in rounds:
            ext[slot] = recvs[rounds.index(here)][...]
        else:
            ext[slot] = jnp.zeros(ext.shape[1:], BF16)

    def slot_of(entry):
        place = entry - tiles
        axis, upper = lax.div(place, 2), lax.rem(place, 2)
        at = jnp.where(axis == 0, lax.axis_index("slabx"), lax.axis_index("slaby"))
        return 2 * axis + 1 - lax.rem(upper + at, 2)

    slots = [[slot_of(index_ref[r, 2]), slot_of(index_ref[r, 3])] for r in range(tiles)]
    chosen = None if final else select_rows(halo_ref, rounds, rows)
    gain = gain_ref[...]
    for b in range(half):
        parts = []
        for r in range(tiles):
            pair = jnp.concatenate([ext[slots[r][0], b], ext[slots[r][1], b]], axis=0)
            edges = jnp.concatenate([values_ref[r, 2], values_ref[r, 3]], axis=1)
            far = dot(edges, pair) + near_ref[b, r * tile : (r + 1) * tile, :]
            parts.append(far.astype(BF16))
        total = jnp.concatenate(parts, axis=0)
        pre = base_ref[b] + dot(total, fold_ref[...])
        act = jnp.maximum(pre, 0.0).astype(BF16)
        out = dot(act, last_ref[...])
        mean = jnp.mean(out, axis=-1, keepdims=True)
        off = out - mean
        var = jnp.mean(off * off, axis=-1, keepdims=True)
        normed = off * lax.rsqrt(var + 1e-05)
        fresh = (state_ref[b].astype(F32) + gain * normed).astype(BF16)
        out_ref[b] = fresh
        if not final:
            sent = dot(chosen, fresh).astype(BF16)
            for n, ref in enumerate(sends):
                ref[b] = sent[n * tile : (n + 1) * tile]


VMEM = pl.BlockSpec(memory_space=pltpu.VMEM)
SMEM = pl.BlockSpec(memory_space=pltpu.SMEM)
HBM = pl.BlockSpec(memory_space=pltpu.HBM)


def shards(nodes, tile_index, tile_values, halo_rows, w_msg, w_in, w_out, bias, gain):
    snaps, rows, width = nodes.shape
    sections = lax.axis_size("section")
    half = snaps // sections
    tiles, _, tile, _ = tile_values.shape
    rounds = meetings([lax.axis_size(name) for name in AXES])
    block = jax.ShapeDtypeStruct((half, tile, width), BF16)
    state_shape = jax.ShapeDtypeStruct((half, rows, width), BF16)
    wide = jax.ShapeDtypeStruct((half, rows, width), F32)
    square = jax.ShapeDtypeStruct((width, width), BF16)
    line = jax.ShapeDtypeStruct((1, width), F32)

    def cost(matmul_rows, nbytes):
        return pl.CostEstimate(
            flops=2 * matmul_rows * width * width, bytes_accessed=nbytes, transcendentals=0
        )

    vec = jnp.concatenate([bias, gain], axis=0)
    mine = (w_msg, w_in, w_out, vec)
    cross = [(0, 1), (1, 0)]
    other = tuple(lax.ppermute(w, "section", cross) for w in mine)

    state, *sends = pl.pallas_call(
        functools.partial(pick_kernel, rounds),
        out_shape=[state_shape] + [block] * len(rounds),
        in_specs=[VMEM, HBM],
        out_specs=[VMEM] * (1 + len(rounds)),
        scratch_shapes=[pltpu.SemaphoreType.DMA((half,))],
        cost_estimate=cost(half * rows, 2 * half * rows * width * 2),
        compiler_params=pltpu.CompilerParams(vmem_limit_bytes=LIMIT),
        name="pick",
    )(halo_rows, nodes)

    for layer in range(2):
        final = layer == 1
        got = [swap(sent, *turn) for sent, turn in zip(sends, rounds)]
        weights = []
        for a, b in zip(mine, other):
            weights += [a, b]
        base, near, fold, last, line_gain = pl.pallas_call(
            functools.partial(local_kernel, layer),
            out_shape=[wide, wide, square, square, line],
            in_specs=[SMEM] + [VMEM] * 10,
            out_specs=[VMEM] * 5,
            cost_estimate=cost(3 * half * rows, 8 * half * rows * width),
            compiler_params=pltpu.CompilerParams(vmem_limit_bytes=LIMIT),
            name=f"local{layer}",
        )(tile_index, tile_values, state, *weights)
        results = pl.pallas_call(
            functools.partial(finish_kernel, rounds, final),
            out_shape=[state_shape] + ([] if final else [block] * len(rounds)),
            in_specs=[SMEM] + [VMEM] * (8 + len(rounds)),
            out_specs=[VMEM] * (1 if final else 1 + len(rounds)),
            scratch_shapes=[pltpu.VMEM((4, half, tile, width), BF16)],
            cost_estimate=cost(3 * half * rows, 8 * half * rows * width),
            compiler_params=pltpu.CompilerParams(vmem_limit_bytes=LIMIT),
            name=f"finish{layer}",
        )(
            tile_index, tile_values, halo_rows, state, base, near, fold, last, line_gain, *got
        )
        state, sends = results[0], results[1:]
    return state


def solution(mesh):
    slab = ("groups", "slabx", "slaby")
    in_specs = (
        P(None, slab, None),
        P(slab, None),
        P(slab, None, None, None),
        P(slab, None, None),
        P("section", None, None),
        P("section", None, None),
        P("section", None, None),
        P("section", None),
        P("section", None),
    )
    out_specs = P("section", slab, None)
    return jax.shard_map(shards, mesh=mesh, in_specs=in_specs, out_specs=out_specs, check_vma=False)
```

time: 159 us -> 35.2 us (0.22); the launches traced: 157 us -> 34.9 us
  starting transfers between devices: 52.3 us -> 12.8 us
  waiting for transfers between devices: 37.5 us -> 6.13 us
  matrix products: 21.1 us -> 0 us
  other arithmetic: 21.2 us -> 0.71 us
  local copies, waits for them, and re-layouts: 20.6 us -> 4.19 us
  Pallas kernels: 0 us -> 11 us
  loops' own time: 4.18 us -> 0 us
    ppermute x26 -> x10, starting transfers between devices: 52.3 us -> 12.8 us  [the longest x6 11.7 us: swap(): return lax.ppermute(block, AXES[axis], route)]
    ppermute x26 -> x10, waiting for transfers between devices: 37.5 us -> 6.13 us  [the longest x6 6.12 us: swap(): return lax.ppermute(block, AXES[axis], route)]
    dot_general x15 -> x0, matrix products: 21.1 us -> none  [the longest x5 11.4 us: layer_step(): jnp.einsum('bnc,ce->bne', act, weight_out, preferred_element_type=jnp.flo...]
    gather x10 -> x0, local copies, waits for them, and re-layouts: 13.1 us -> none  [the longest x5 9.86 us: layer_step(): picked = jnp.take(msg, halo_rows[0], axis=1)]
    select_n x21 -> x0, other arithmetic: 11.4 us -> none  [the longest x5 5.22 us: one_tick(): current = jnp.where(section_id == 0, fresh, received)]
    pallas_call x0 -> x5, Pallas kernels: none -> 11 us  [the longest x2 6.33 us: shards(): pl.pallas_call(functools.partial(finish_kernel, rounds, final), out_shape...]
    dynamic_update_slice x5 -> x0, other arithmetic: 4.95 us -> none  [shards(): lax.scan(one_tick, start, jnp.arange(snaps + 1, dtype=jnp.int32))]
    unnamed x0 -> x20, local copies, waits for them, and re-layouts: none -> 4.19 us
  transfers between devices with their start and end apart: 26 -> 10, of which waited for: 17 -> 4; matrix products, arithmetic and copies ran while one was open for 1% -> 2% of each run, Pallas kernels for 0% -> 13%
where the time goes in v1:
time: 35.2 us; the launch traced here: 34.9 us
  starting transfers between devices  12.8 us (36%)
  Pallas kernels  11 us (31%)
  waiting for transfers between devices  6.13 us (17%)
  local copies, waits for them, and re-layouts  4.19 us (12%)
  other arithmetic  0.71 us (2%)
    ppermute x6, starting transfers between devices, swap(): return lax.ppermute(block, AXES[axis], route)  11.7 us
    pallas_call x2, Pallas kernels, shards(): pl.pallas_call(functools.partial(finish_kernel, rounds, final), out_shape...  6.33 us
    ppermute x6, waiting for transfers between devices, swap(): return lax.ppermute(block, AXES[axis], route)  6.12 us
    unnamed x20, local copies, waits for them, and re-layouts  4.19 us
    pallas_call x2, Pallas kernels, shards(): pl.pallas_call(functools.partial(local_kernel, layer), out_shape=[wide, w...  3.34 us
    pallas_call x1, Pallas kernels, shards(): pl.pallas_call(functools.partial(pick_kernel, rounds), out_shape=[state_s...  1.29 us
    ppermute x4, starting transfers between devices, shards(): other = tuple((lax.ppermute(w, 'section', cross) for w in mine))  1.13 us
    concatenate x1, other arithmetic, shards(): vec = jnp.concatenate([bias, gain], axis=0)  0.71 us
  transfers between devices with their start and end apart: 10, of which 4 were waited for; matrix products, arithmetic and copies ran while one was open for 2% of the time, Pallas kernels for 13%

profile of v1, /device:TPU:0, one launch (start us, length us, event | category | flops | bytes accessed | tf_op | source)
XLA Modules:
  0.0 34.9 jit_solution(1588060874680244659)
XLA Ops:
  0.0 0.5 %collective-permute-start.1 = (bf16[1,1024,512]{2,1,0:T(8,128)(2,1)}, bf16[1,1024,512]{2,1,0:T(8,128)(2,1)S(1)}, u32[]{:S(2)}, u32[]{:S(2)}) collective-permute-start(bf16[1,1024,512]{2,1,0:T(8,128)(2,1)} %in_a.3), channel_id=1, source_target_pairs={{0,1},{1,0},{2,3},{3,2},{4,5},{5,4},{6,7},{7,6},{8,9},{9,8},{10,11... | collective-permute-start | bytes 3145736 | tf_op jit(solution)/shard_map/ppermute | solution.py:179
  0.5 0.1 collective-permute-start
  0.6 0.4 %collective-permute-start.2 = (bf16[1,512,512]{2,1,0:T(8,128)(2,1)}, bf16[1,512,512]{2,1,0:T(8,128)(2,1)S(1)}, u32[]{:S(2)}, u32[]{:S(2)}) collective-permute-start(bf16[1,512,512]{2,1,0:T(8,128)(2,1)} %out_a.3), channel_id=1, source_target_pairs={{0,1},{1,0},{2,3},{3,2},{4,5},{5,4},{6,7},{7,6},{8,9},{9,8},{10,11... | collective-permute-start | bytes 1572872 | tf_op jit(solution)/shard_map/ppermute | solution.py:179
  1.0 0.7 %pad_maximum_fusion.vec_a = f32[2,512]{1,0:T(2,128)S(1)} fusion(f32[1,512]{1,0:T(1,128)} %param.17, f32[1,512]{1,0:T(1,128)} %param.16), kind=kLoop, calls=%fused_computation | loop fusion | flops 1024 | bytes 8192 | tf_op jit(solution)/shard_map/concatenate | solution.py:176
  1.7 0.1 collective-permute-start.3
  1.8 1.4 %copy-done.6 = bf16[4,384,512]{2,1,0:T(8,128)(2,1)S(1)} copy-done((bf16[4,384,512]{2,1,0:T(8,128)(2,1)S(1)}, bf16[4,384,512]{2,1,0:T(8,128)(2,1)}, u32[]{:S(2)}) %copy-start.6) | copy-done | bytes 1572888
  3.3 0.7 %copy-done.8 = s32[1,4,128]{2,1,0:T(4,128)S(1)} copy-done((s32[1,4,128]{2,1,0:T(4,128)S(1)}, s32[1,4,128]{2,1,0:T(4,128)}, u32[]{:S(2)}) %copy-start.8) | copy-done | bytes 2072
  3.9 1.3 %pick.1 = (bf16[2,384,512]{2,1,0:T(8,128)(2,1)S(1)}, bf16[2,128,512]{2,1,0:T(8,128)(2,1)S(1)}, bf16[2,128,512]{2,1,0:T(8,128)(2,1)S(1)}, bf16[2,128,512]{2,1,0:T(8,128)(2,1)S(1)}) custom-call(s32[1,4,128]{2,1,0:T(4,128)S(1)} %copy-done.8, bf16[4,384,512]{2,1,0:T(8,128)(2,1)S(1)} %copy-done.6), custom_call_target="tpu_custom_call" | custom-call | flops 402653184 | bytes 1572864 | tf_op jit(solution)/shard_map/pick/pallas_call | solution.py:181
  5.2 3.1 %collective-permute-start.4 = (bf16[2,128,512]{2,1,0:T(8,128)(2,1)S(1)}, bf16[2,128,512]{2,1,0:T(8,128)(2,1)S(1)}, u32[]{:S(2)}, u32[]{:S(2)}) collective-permute-start(bf16[2,128,512]{2,1,0:T(8,128)(2,1)S(1)} %get-tuple-element.29), channel_id=1, source_target_pairs={{0,4},{4,0},{8,12},{12,8},{1,5},{5,1},{9,13},{13,9},{2,6},{6,2},{1... | collective-permute-start | bytes 786440 | tf_op jit(solution)/shard_map/ppermute | solution.py:29
  8.3 0.0 collective-permute-done.3.vec_b
  8.3 0.7 %collective-permute-start.5 = (bf16[2,128,512]{2,1,0:T(8,128)(2,1)S(1)}, bf16[2,128,512]{2,1,0:T(8,128)(2,1)S(1)}, u32[]{:S(2)}, u32[]{:S(2)}) collective-permute-start(bf16[2,128,512]{2,1,0:T(8,128)(2,1)S(1)} %get-tuple-element.30), channel_id=1, source_target_pairs={{4,8},{8,4},{5,9},{9,5},{6,10},{10,6},{7,11},{11,7},{20,24},{24,20... | collective-permute-start | bytes 786440 | tf_op jit(solution)/shard_map/ppermute | solution.py:29
  9.0 0.0 collective-permute-done.msg_b
  9.0 1.6 %collective-permute-start.6 = (bf16[2,128,512]{2,1,0:T(8,128)(2,1)S(1)}, bf16[2,128,512]{2,1,0:T(8,128)(2,1)S(1)}, u32[]{:S(2)}, u32[]{:S(2)}) collective-permute-start(bf16[2,128,512]{2,1,0:T(8,128)(2,1)S(1)} %get-tuple-element.31), channel_id=1, source_target_pairs={{0,2},{2,0},{1,3},{3,1},{4,6},{6,4},{5,7},{7,5},{8,10},{10,8},{9,1... | collective-permute-start | bytes 786440 | tf_op jit(solution)/shard_map/ppermute | solution.py:29
  10.5 0.0 collective-permute-done.2.out_b
  10.5 0.0 collective-permute-done.1.in_b
  10.5 0.0 copy-done
  10.6 0.0 copy-start.2
  10.6 1.0 %copy-done.2 = bf16[1,512,512]{2,1,0:T(8,128)(2,1)S(1)} copy-done((bf16[1,512,512]{2,1,0:T(8,128)(2,1)S(1)}, bf16[1,512,512]{2,1,0:T(8,128)(2,1)}, u32[]{:S(2)}) %copy-start.2) | copy-done | bytes 524312
  11.6 1.0 %copy-done.4 = bf16[1,512,512]{2,1,0:T(8,128)(2,1)S(1)} copy-done((bf16[1,512,512]{2,1,0:T(8,128)(2,1)S(1)}, bf16[1,512,512]{2,1,0:T(8,128)(2,1)}, u32[]{:S(2)}) %copy-start.4) | copy-done | bytes 524312
  12.7 1.7 %local0.1 = (f32[2,384,512]{2,1,0:T(8,128)S(1)}, f32[2,384,512]{2,1,0:T(8,128)S(1)}, bf16[512,512]{1,0:T(8,128)(2,1)S(1)}, bf16[512,512]{1,0:T(8,128)(2,1)S(1)}, f32[1,512]{1,0:T(1,128)S(1)}) custom-call(s32[3,4]{1,0:T(4,128)S(1)} %copy-done.7, bf16[3,4,128,128]{3,2,1,0:T(8,128)(2,1)S(1)} %copy-done, bf16[2,384,512]{2,1,0:T(8,128)(2,1)S(1)} %get-tuple-element.23.state_ref, ...), custom_call_target="tpu_custom_call" | custom-call | flops 1207959552 | bytes 3145728 | tf_op jit(solution)/shard_map/local0/pallas_call | solution.py:198
  14.3 0.5 %collective-permute-done.4.rest_0_ = bf16[2,128,512]{2,1,0:T(8,128)(2,1)S(1)} collective-permute-done((bf16[2,128,512]{2,1,0:T(8,128)(2,1)S(1)}, bf16[2,128,512]{2,1,0:T(8,128)(2,1)S(1)}, u32[]{:S(2)}, u32[]{:S(2)}) %collective-permute-start.4) | collective-permute-done | bytes 262176 | tf_op jit(solution)/shard_map/ppermute | solution.py:29
  14.8 0.0 collective-permute-done.5.rest_1_
  14.8 2.2 %collective-permute-done.6.rest_2_ = bf16[2,128,512]{2,1,0:T(8,128)(2,1)S(1)} collective-permute-done((bf16[2,128,512]{2,1,0:T(8,128)(2,1)S(1)}, bf16[2,128,512]{2,1,0:T(8,128)(2,1)S(1)}, u32[]{:S(2)}, u32[]{:S(2)}) %collective-permute-start.6) | collective-permute-done | bytes 262176 | tf_op jit(solution)/shard_map/ppermute | solution.py:29
  17.0 3.1 %finish0.1 = (bf16[2,384,512]{2,1,0:T(8,128)(2,1)S(1)}, bf16[2,128,512]{2,1,0:T(8,128)(2,1)S(1)}, bf16[2,128,512]{2,1,0:T(8,128)(2,1)S(1)}, bf16[2,128,512]{2,1,0:T(8,128)(2,1)S(1)}) custom-call(s32[3,4]{1,0:T(4,128)S(1)} %copy-done.7, bf16[3,4,128,128]{3,2,1,0:T(8,128)(2,1)S(1)} %copy-done, s32[1,4,128]{2,1,0:T(4,128)S(1)} %copy-done.9, ...), custom_call_target="tpu_custom_call" | custom-call | flops 1207959552 | bytes 3145728 | tf_op jit(solution)/shard_map/finish0/pallas_call | solution.py:207
  20.2 4.2 %collective-permute-start.7 = (bf16[2,128,512]{2,1,0:T(8,128)(2,1)S(1)}, bf16[2,128,512]{2,1,0:T(8,128)(2,1)S(1)}, u32[]{:S(2)}, u32[]{:S(2)}) collective-permute-start(bf16[2,128,512]{2,1,0:T(8,128)(2,1)S(1)} %get-tuple-element.38), channel_id=1, source_target_pairs={{0,4},{4,0},{8,12},{12,8},{1,5},{5,1},{9,13},{13,9},{2,6},{6,2},{1... | collective-permute-start | bytes 786440 | tf_op jit(solution)/shard_map/ppermute | solution.py:29
  24.4 0.7 %collective-permute-start.8 = (bf16[2,128,512]{2,1,0:T(8,128)(2,1)S(1)}, bf16[2,128,512]{2,1,0:T(8,128)(2,1)S(1)}, u32[]{:S(2)}, u32[]{:S(2)}) collective-permute-start(bf16[2,128,512]{2,1,0:T(8,128)(2,1)S(1)} %get-tuple-element.39), channel_id=1, source_target_pairs={{4,8},{8,4},{5,9},{9,5},{6,10},{10,6},{7,11},{11,7},{20,24},{24,20... | collective-permute-start | bytes 786440 | tf_op jit(solution)/shard_map/ppermute | solution.py:29
  25.0 1.6 %collective-permute-start.9 = (bf16[2,128,512]{2,1,0:T(8,128)(2,1)S(1)}, bf16[2,128,512]{2,1,0:T(8,128)(2,1)S(1)}, u32[]{:S(2)}, u32[]{:S(2)}) collective-permute-start(bf16[2,128,512]{2,1,0:T(8,128)(2,1)S(1)} %get-tuple-element.40), channel_id=1, source_target_pairs={{0,2},{2,0},{1,3},{3,1},{4,6},{6,4},{5,7},{7,5},{8,10},{10,8},{9,1... | collective-permute-start | bytes 786440 | tf_op jit(solution)/shard_map/ppermute | solution.py:29
  26.6 1.7 %local1.1 = (f32[2,384,512]{2,1,0:T(8,128)S(1)}, f32[2,384,512]{2,1,0:T(8,128)S(1)}, bf16[512,512]{1,0:T(8,128)(2,1)S(1)}, bf16[512,512]{1,0:T(8,128)(2,1)S(1)}, f32[1,512]{1,0:T(1,128)S(1)}) custom-call(s32[3,4]{1,0:T(4,128)S(1)} %copy-done.7, bf16[3,4,128,128]{3,2,1,0:T(8,128)(2,1)S(1)} %copy-done, bf16[2,384,512]{2,1,0:T(8,128)(2,1)S(1)} %get-tuple-element.32.state_ref, ...), custom_call_target="tpu_custom_call" | custom-call | flops 1207959552 | bytes 3145728 | tf_op jit(solution)/shard_map/local1/pallas_call | solution.py:198
  28.3 1.2 %collective-permute-done.7.rest_0_ = bf16[2,128,512]{2,1,0:T(8,128)(2,1)S(1)} collective-permute-done((bf16[2,128,512]{2,1,0:T(8,128)(2,1)S(1)}, bf16[2,128,512]{2,1,0:T(8,128)(2,1)S(1)}, u32[]{:S(2)}, u32[]{:S(2)}) %collective-permute-start.7) | collective-permute-done | bytes 262176 | tf_op jit(solution)/shard_map/ppermute | solution.py:29
  29.5 0.0 collective-permute-done.8.rest_1_
  29.5 2.2 %collective-permute-done.9.rest_2_ = bf16[2,128,512]{2,1,0:T(8,128)(2,1)S(1)} collective-permute-done((bf16[2,128,512]{2,1,0:T(8,128)(2,1)S(1)}, bf16[2,128,512]{2,1,0:T(8,128)(2,1)S(1)}, u32[]{:S(2)}, u32[]{:S(2)}) %collective-permute-start.9) | collective-permute-done | bytes 262176 | tf_op jit(solution)/shard_map/ppermute | solution.py:29
  31.7 3.2 %finish1.1 = bf16[2,384,512]{2,1,0:T(8,128)(2,1)} custom-call(s32[3,4]{1,0:T(4,128)S(1)} %copy-done.7, bf16[3,4,128,128]{3,2,1,0:T(8,128)(2,1)S(1)} %copy-done, s32[1,4,128]{2,1,0:T(4,128)S(1)} %copy-done.9, bf16[2,384,512]{2,1,0:T(8,128)(2,1)S(1)} %get-tuple-element.32.state_ref, f32[2,384,512]{2,1,0:T(8,128)S(1)} %get-tuple-element.33.base_ref, ...), custom_call_target="tpu_custom_call" | custom-call | flops 1207959552 | bytes 3145728 | tf_op jit(solution)/shard_map/finish1/pallas_call | solution.py:207
  (14 shorter events, 0.0 us)
Async XLA Ops:
  0.0 10.5 %copy-start.1 = (bf16[1,1024,512]{2,1,0:T(8,128)(2,1)S(1)}, bf16[1,1024,512]{2,1,0:T(8,128)(2,1)}, u32[]{:S(2)}) copy-start(bf16[1,1024,512]{2,1,0:T(8,128)(2,1)} %in_a.3) | copy-start | bytes 3145732
  0.0 10.5 %copy-start = (bf16[3,4,128,128]{3,2,1,0:T(8,128)(2,1)S(1)}, bf16[3,4,128,128]{3,2,1,0:T(8,128)(2,1)}, u32[]{:S(2)}) copy-start(bf16[3,4,128,128]{3,2,1,0:T(8,128)(2,1)} %values_ref.7) | copy-start | bytes 1179652
  0.0 10.5 %collective-permute-start.1 = (bf16[1,1024,512]{2,1,0:T(8,128)(2,1)}, bf16[1,1024,512]{2,1,0:T(8,128)(2,1)S(1)}, u32[]{:S(2)}, u32[]{:S(2)}) collective-permute-start(bf16[1,1024,512]{2,1,0:T(8,128)(2,1)} %in_a.3), channel_id=1, source_target_pairs={{0,1},{1,0},{2,3},{3,2},{4,5},{5,4},{6,7},{7,6},{8,9},{9,8},{10,11... | collective-permute-start | bytes 3145736 | tf_op jit(solution)/shard_map/ppermute | solution.py:179
  0.5 8.5 %collective-permute-start = (bf16[1,512,512]{2,1,0:T(8,128)(2,1)}, bf16[1,512,512]{2,1,0:T(8,128)(2,1)S(1)}, u32[]{:S(2)}, u32[]{:S(2)}) collective-permute-start(bf16[1,512,512]{2,1,0:T(8,128)(2,1)} %msg_a.3), channel_id=1, source_target_pairs={{0,1},{1,0},{2,3},{3,2},{4,5},{5,4},{6,7},{7,6},{8,9},{9,8},{10,11... | collective-permute-start | bytes 1572872 | tf_op jit(solution)/shard_map/ppermute | solution.py:179
  0.6 10.0 %collective-permute-start.2 = (bf16[1,512,512]{2,1,0:T(8,128)(2,1)}, bf16[1,512,512]{2,1,0:T(8,128)(2,1)S(1)}, u32[]{:S(2)}, u32[]{:S(2)}) collective-permute-start(bf16[1,512,512]{2,1,0:T(8,128)(2,1)} %out_a.3), channel_id=1, source_target_pairs={{0,1},{1,0},{2,3},{3,2},{4,5},{5,4},{6,7},{7,6},{8,9},{9,8},{10,11... | collective-permute-start | bytes 1572872 | tf_op jit(solution)/shard_map/ppermute | solution.py:179
  1.7 6.6 %collective-permute-start.3 = (f32[2,512]{1,0:T(2,128)S(1)}, f32[2,512]{1,0:T(2,128)S(1)}, u32[]{:S(2)}, u32[]{:S(2)}) collective-permute-start(f32[2,512]{1,0:T(2,128)S(1)} %pad_maximum_fusion.vec_a), channel_id=1, source_target_pairs={{0,1},{1,0},{2,3},{3,2},{4,5},{5,4},{6,7},{7,6},{8,9},{9,8},{10,11... | collective-permute-start | bytes 12296 | tf_op jit(solution)/shard_map/ppermute | solution.py:179
  1.8 1.4 %copy-start.6 = (bf16[4,384,512]{2,1,0:T(8,128)(2,1)S(1)}, bf16[4,384,512]{2,1,0:T(8,128)(2,1)}, u32[]{:S(2)}) copy-start(bf16[4,384,512]{2,1,0:T(8,128)(2,1)} %nodes_ref.1) | copy-start | bytes 4718596
  3.2 0.7 %copy-start.8 = (s32[1,4,128]{2,1,0:T(4,128)S(1)}, s32[1,4,128]{2,1,0:T(4,128)}, u32[]{:S(2)}) copy-start(s32[1,4,128]{2,1,0:T(4,128)} %halo_ref.5) | copy-start | bytes 6148
  3.9 6.6 %copy-start.7 = (s32[3,4]{1,0:T(4,128)S(1)}, s32[3,4]{1,0:T(4,128)}, u32[]{:S(2)}) copy-start(s32[3,4]{1,0:T(4,128)} %index_ref.7) | copy-start | bytes 148
  5.2 9.6 %collective-permute-start.4 = (bf16[2,128,512]{2,1,0:T(8,128)(2,1)S(1)}, bf16[2,128,512]{2,1,0:T(8,128)(2,1)S(1)}, u32[]{:S(2)}, u32[]{:S(2)}) collective-permute-start(bf16[2,128,512]{2,1,0:T(8,128)(2,1)S(1)} %get-tuple-element.29), channel_id=1, source_target_pairs={{0,4},{4,0},{8,12},{12,8},{1,5},{5,1},{9,13},{13,9},{2,6},{6,2},{1... | collective-permute-start | bytes 786440 | tf_op jit(solution)/shard_map/ppermute | solution.py:29
  8.3 6.5 %collective-permute-start.5 = (bf16[2,128,512]{2,1,0:T(8,128)(2,1)S(1)}, bf16[2,128,512]{2,1,0:T(8,128)(2,1)S(1)}, u32[]{:S(2)}, u32[]{:S(2)}) collective-permute-start(bf16[2,128,512]{2,1,0:T(8,128)(2,1)S(1)} %get-tuple-element.30), channel_id=1, source_target_pairs={{4,8},{8,4},{5,9},{9,5},{6,10},{10,6},{7,11},{11,7},{20,24},{24,20... | collective-permute-start | bytes 786440 | tf_op jit(solution)/shard_map/ppermute | solution.py:29
  9.0 8.1 %collective-permute-start.6 = (bf16[2,128,512]{2,1,0:T(8,128)(2,1)S(1)}, bf16[2,128,512]{2,1,0:T(8,128)(2,1)S(1)}, u32[]{:S(2)}, u32[]{:S(2)}) collective-permute-start(bf16[2,128,512]{2,1,0:T(8,128)(2,1)S(1)} %get-tuple-element.31), channel_id=1, source_target_pairs={{0,2},{2,0},{1,3},{3,1},{4,6},{6,4},{5,7},{7,5},{8,10},{10,8},{9,1... | collective-permute-start | bytes 786440 | tf_op jit(solution)/shard_map/ppermute | solution.py:29
  10.6 1.0 %copy-start.2 = (bf16[1,512,512]{2,1,0:T(8,128)(2,1)S(1)}, bf16[1,512,512]{2,1,0:T(8,128)(2,1)}, u32[]{:S(2)}) copy-start(bf16[1,512,512]{2,1,0:T(8,128)(2,1)} %msg_a.3) | copy-start | bytes 1572868
  11.6 1.0 %copy-start.4 = (bf16[1,512,512]{2,1,0:T(8,128)(2,1)S(1)}, bf16[1,512,512]{2,1,0:T(8,128)(2,1)}, u32[]{:S(2)}) copy-start(bf16[1,512,512]{2,1,0:T(8,128)(2,1)} %out_a.3) | copy-start | bytes 1572868
  12.7 4.4 %copy-start.9 = (s32[1,4,128]{2,1,0:T(4,128)S(1)}, s32[1,4,128]{2,1,0:T(4,128)}, u32[]{:S(2)}) copy-start(s32[1,4,128]{2,1,0:T(4,128)} %halo_ref.5) | copy-start | bytes 6148
  17.0 9.6 %copy-start.3 = (bf16[1,512,512]{2,1,0:T(8,128)(2,1)S(1)}, bf16[1,512,512]{2,1,0:T(8,128)(2,1)}, u32[]{:S(2)}) copy-start(bf16[1,512,512]{2,1,0:T(8,128)(2,1)} %msg_a.3) | copy-start | bytes 1572868
  17.0 9.6 %copy-start.5 = (bf16[1,512,512]{2,1,0:T(8,128)(2,1)S(1)}, bf16[1,512,512]{2,1,0:T(8,128)(2,1)}, u32[]{:S(2)}) copy-start(bf16[1,512,512]{2,1,0:T(8,128)(2,1)} %out_a.3) | copy-start | bytes 1572868
  20.2 9.3 %collective-permute-start.7 = (bf16[2,128,512]{2,1,0:T(8,128)(2,1)S(1)}, bf16[2,128,512]{2,1,0:T(8,128)(2,1)S(1)}, u32[]{:S(2)}, u32[]{:S(2)}) collective-permute-start(bf16[2,128,512]{2,1,0:T(8,128)(2,1)S(1)} %get-tuple-element.38), channel_id=1, source_target_pairs={{0,4},{4,0},{8,12},{12,8},{1,5},{5,1},{9,13},{13,9},{2,6},{6,2},{1... | collective-permute-start | bytes 786440 | tf_op jit(solution)/shard_map/ppermute | solution.py:29
  24.4 5.1 %collective-permute-start.8 = (bf16[2,128,512]{2,1,0:T(8,128)(2,1)S(1)}, bf16[2,128,512]{2,1,0:T(8,128)(2,1)S(1)}, u32[]{:S(2)}, u32[]{:S(2)}) collective-permute-start(bf16[2,128,512]{2,1,0:T(8,128)(2,1)S(1)} %get-tuple-element.39), channel_id=1, source_target_pairs={{4,8},{8,4},{5,9},{9,5},{6,10},{10,6},{7,11},{11,7},{20,24},{24,20... | collective-permute-start | bytes 786440 | tf_op jit(solution)/shard_map/ppermute | solution.py:29
  25.0 6.7 %collective-permute-start.9 = (bf16[2,128,512]{2,1,0:T(8,128)(2,1)S(1)}, bf16[2,128,512]{2,1,0:T(8,128)(2,1)S(1)}, u32[]{:S(2)}, u32[]{:S(2)}) collective-permute-start(bf16[2,128,512]{2,1,0:T(8,128)(2,1)S(1)} %get-tuple-element.40), channel_id=1, source_target_pairs={{0,2},{2,0},{1,3},{3,1},{4,6},{6,4},{5,7},{7,5},{8,10},{10,8},{9,1... | collective-permute-start | bytes 786440 | tf_op jit(solution)/shard_map/ppermute | solution.py:29

commit v2 on v1

--- a/solution.py
+++ b/solution.py
@@ -18,7 +18,7 @@
 
 
 def meetings(sizes):
-    return [(axis, turn) for axis in range(2) for turn in range(2) if sizes[axis] > 1 + turn]
+    return [(axis, turn) for axis in range(2) for turn in (1, 0) if sizes[axis] > 1 + turn]
 
 
 def swap(block, axis, turn):
@@ -50,16 +50,19 @@
     )
 
 
-def pick_kernel(rounds, halo_ref, nodes_ref, state_ref, *rest):
-    sends, (sem,) = rest[: len(rounds)], rest[len(rounds) :]
+def pick_kernel(rounds, halo_hbm, nodes_ref, state_ref, *rest):
+    sends, (halo_ref, sem) = rest[: len(rounds)], rest[len(rounds) :]
     half, rows, _ = state_ref.shape
     section = lax.axis_index("section")
+    lists = pltpu.make_async_copy(halo_hbm, halo_ref, sem.at[half])
+    lists.start()
     fetch = [
         pltpu.make_async_copy(nodes_ref.at[section * half + b], state_ref.at[b], sem.at[b])
         for b in range(half)
     ]
     for copy in fetch:
         copy.start()
+    lists.wait()
     chosen = select_rows(halo_ref, rounds, rows)
     count = chosen.shape[0] // len(rounds)
     for b in range(half):
@@ -69,37 +72,51 @@
             ref[b] = sent[n * count : (n + 1) * count]
 
 
-def local_work(index_ref, values_ref, state, w_in, w_msg, bias, half, base_ref, near_ref, fold_ref):
-    tiles, _, tile, _ = values_ref.shape
-    width = w_msg.shape[0]
-    top, bottom = w_in[:width], w_in[width:]
-    fold_ref[...] = dot(w_msg, bottom).astype(BF16)
-    for b in range(half):
-        base_ref[b] = dot(state[b], top) + bias
-        for r in range(tiles):
-            other = pl.multiple_of(index_ref[r, 1] * tile, tile)
-            pair = jnp.concatenate(
-                [state[b, r * tile : (r + 1) * tile, :], state[b, pl.ds(other, tile), :]], axis=0
-            )
-            edges = jnp.concatenate([values_ref[r, 0], values_ref[r, 1]], axis=1)
-            near_ref[b, r * tile : (r + 1) * tile, :] = dot(edges, pair)
-
-
 def local_kernel(
     layer, index_ref, values_ref, state_ref,
-    msg_a, msg_b, in_a, in_b, out_a, out_b, vec_a, vec_b,
-    base_ref, near_ref, fold_ref, last_ref, gain_ref,
+    msg_a, msg_b, in_a, in_b, out_a, out_b, bias_a, bias_b, gain_a, gain_b,
+    base_ref, near_ref, fold_ref, last_ref, gain_ref, msg_ref, in_ref, sem,
 ):
     mine = lax.axis_index("section") == layer
     half = base_ref.shape[0]
-    pick = lambda a, b: jnp.where(mine, a[...], b[...])
-    vec = pick(vec_a, vec_b)
-    gain_ref[...] = vec[1:2]
-    last_ref[...] = pick(out_a, out_b)[0]
-    local_work(
-        index_ref, values_ref, state_ref, pick(in_a, in_b)[0], pick(msg_a, msg_b)[0], vec[0:1],
-        half, base_ref, near_ref, fold_ref,
-    )
+    tiles, _, tile, _ = values_ref.shape
+    width = last_ref.shape[0]
+    into = (msg_ref, in_ref, last_ref)
+    kept = [
+        pltpu.make_async_copy(w.at[0], ref, sem.at[n])
+        for n, (w, ref) in enumerate(zip((msg_a, in_a, out_a), into))
+    ]
+    came = [
+        pltpu.make_async_copy(w.at[0], ref, sem.at[n])
+        for n, (w, ref) in enumerate(zip((msg_b, in_b, out_b), into))
+    ]
+
+    @pl.when(mine)
+    def _():
+        for copy in kept:
+            copy.start()
+
+    @pl.when(jnp.logical_not(mine))
+    def _():
+        for copy in came:
+            copy.start()
+
+    gain_ref[...] = jnp.where(mine, gain_a[...], gain_b[...])
+    bias = jnp.where(mine, bias_a[...], bias_b[...])
+    for r in range(tiles):
+        other = pl.multiple_of(index_ref[r, 1] * tile, tile)
+        edges = jnp.concatenate([values_ref[r, 0], values_ref[r, 1]], axis=1)
+        for b in range(half):
+            pair = jnp.concatenate(
+                [state_ref[b, r * tile : (r + 1) * tile, :], state_ref[b, pl.ds(other, tile), :]],
+                axis=0,
+            )
+            near_ref[b, r * tile : (r + 1) * tile, :] = dot(edges, pair)
+    for copy in kept:
+        copy.wait()
+    fold_ref[...] = dot(msg_ref[...], in_ref[width:]).astype(BF16)
+    for b in range(half):
+        base_ref[b] = dot(state_ref[b], in_ref[:width]) + bias
 
 
 def finish_kernel(
@@ -109,7 +126,7 @@
     recvs, rest = rest[: len(rounds)], rest[len(rounds) :]
     out_ref, rest = rest[0], rest[1:]
     sends, rest = ((), rest) if final else (rest[: len(rounds)], rest[len(rounds) :])
-    ext = rest[0]
+    ext, rest = rest[0], rest[1:]
     half, rows, width = base_ref.shape
     tiles, _, tile, _ = values_ref.shape
     for slot in range(4):
@@ -126,8 +143,8 @@
         return 2 * axis + 1 - lax.rem(upper + at, 2)
 
     slots = [[slot_of(index_ref[r, 2]), slot_of(index_ref[r, 3])] for r in range(tiles)]
-    chosen = None if final else select_rows(halo_ref, rounds, rows)
     gain = gain_ref[...]
+    acts, outs = [], []
     for b in range(half):
         parts = []
         for r in range(tiles):
@@ -137,18 +154,30 @@
             parts.append(far.astype(BF16))
         total = jnp.concatenate(parts, axis=0)
         pre = base_ref[b] + dot(total, fold_ref[...])
-        act = jnp.maximum(pre, 0.0).astype(BF16)
-        out = dot(act, last_ref[...])
+        acts.append(jnp.maximum(pre, 0.0).astype(BF16))
+    for b in range(half):
+        outs.append(dot(acts[b], last_ref[...]))
+    chosen = None if final else select_rows(halo_ref, rounds, rows)
+    writes = []
+    for b in range(half):
+        out = outs[b]
         mean = jnp.mean(out, axis=-1, keepdims=True)
         off = out - mean
         var = jnp.mean(off * off, axis=-1, keepdims=True)
         normed = off * lax.rsqrt(var + 1e-05)
         fresh = (state_ref[b].astype(F32) + gain * normed).astype(BF16)
-        out_ref[b] = fresh
-        if not final:
+        if final:
+            done, sem = rest
+            done[b] = fresh
+            writes.append(pltpu.make_async_copy(done.at[b], out_ref.at[b], sem.at[b]))
+            writes[b].start()
+        else:
+            out_ref[b] = fresh
             sent = dot(chosen, fresh).astype(BF16)
             for n, ref in enumerate(sends):
                 ref[b] = sent[n * tile : (n + 1) * tile]
+    for copy in writes:
+        copy.wait()
 
 
 VMEM = pl.BlockSpec(memory_space=pltpu.VMEM)
@@ -173,33 +202,40 @@
             flops=2 * matmul_rows * width * width, bytes_accessed=nbytes, transcendentals=0
         )
 
-    vec = jnp.concatenate([bias, gain], axis=0)
-    mine = (w_msg, w_in, w_out, vec)
+    mine = (w_msg, w_in, w_out, bias, gain)
     cross = [(0, 1), (1, 0)]
     other = tuple(lax.ppermute(w, "section", cross) for w in mine)
 
     state, *sends = pl.pallas_call(
         functools.partial(pick_kernel, rounds),
         out_shape=[state_shape] + [block] * len(rounds),
-        in_specs=[VMEM, HBM],
+        in_specs=[HBM, HBM],
         out_specs=[VMEM] * (1 + len(rounds)),
-        scratch_shapes=[pltpu.SemaphoreType.DMA((half,))],
+        scratch_shapes=[
+            pltpu.VMEM(halo_rows.shape, jnp.int32),
+            pltpu.SemaphoreType.DMA((half + 1,)),
+        ],
         cost_estimate=cost(half * rows, 2 * half * rows * width * 2),
         compiler_params=pltpu.CompilerParams(vmem_limit_bytes=LIMIT),
         name="pick",
-    )(halo_rows, nodes)
+    )(pltpu.with_memory_space_constraint(halo_rows, pltpu.HBM), pltpu.with_memory_space_constraint(nodes, pltpu.HBM))
 
     for layer in range(2):
         final = layer == 1
         got = [swap(sent, *turn) for sent, turn in zip(sends, rounds)]
         weights = []
-        for a, b in zip(mine, other):
-            weights += [a, b]
+        for n, (a, b) in enumerate(zip(mine, other)):
+            weights += [pltpu.with_memory_space_constraint(a, pltpu.HBM) if n < 3 else a, b]
         base, near, fold, last, line_gain = pl.pallas_call(
             functools.partial(local_kernel, layer),
             out_shape=[wide, wide, square, square, line],
-            in_specs=[SMEM] + [VMEM] * 10,
+            in_specs=[SMEM] + [VMEM] * 2 + [HBM, VMEM] * 3 + [VMEM] * 4,
             out_specs=[VMEM] * 5,
+            scratch_shapes=[
+                pltpu.VMEM((width, width), BF16),
+                pltpu.VMEM((2 * width, width), BF16),
+                pltpu.SemaphoreType.DMA((3,)),
+            ],
             cost_estimate=cost(3 * half * rows, 8 * half * rows * width),
             compiler_params=pltpu.CompilerParams(vmem_limit_bytes=LIMIT),
             name=f"local{layer}",
@@ -208,8 +244,13 @@
             functools.partial(finish_kernel, rounds, final),
             out_shape=[state_shape] + ([] if final else [block] * len(rounds)),
             in_specs=[SMEM] + [VMEM] * (8 + len(rounds)),
-            out_specs=[VMEM] * (1 if final else 1 + len(rounds)),
-            scratch_shapes=[pltpu.VMEM((4, half, tile, width), BF16)],
+            out_specs=[HBM] if final else [VMEM] * (1 + len(rounds)),
+            scratch_shapes=[pltpu.VMEM((4, half, tile, width), BF16)]
+            + (
+                [pltpu.VMEM((half, rows, width), BF16), pltpu.SemaphoreType.DMA((half,))]
+                if final
+                else []
+            ),
             cost_estimate=cost(3 * half * rows, 8 * half * rows * width),
             compiler_params=pltpu.CompilerParams(vmem_limit_bytes=LIMIT),
             name=f"finish{layer}",

time: 35.2 us -> 34.1 us (0.969)
  local copies, waits for them, and re-layouts: 4.19 us -> 0.02 us
  waiting for transfers between devices: 6.13 us -> 7.62 us
  Pallas kernels: 11 us -> 12.4 us
  starting transfers between devices: 12.8 us -> 13.8 us
  other arithmetic: 0.71 us -> 0 us
    unnamed x20 -> x10, local copies, waits for them, and re-layouts: 4.19 us -> 0.02 us
    pallas_call x2, Pallas kernels: 3.34 us -> 4.95 us  [shards(): pl.pallas_call(functools.partial(local_kernel, layer), out_shape=[wide, w...]
    ppermute x4 -> x5, waiting for transfers between devices: 0.01 us -> 1.21 us  [shards(): other = tuple((lax.ppermute(w, 'section', cross) for w in mine))]
    concatenate x1 -> x0, other arithmetic: 0.71 us -> none  [shards(): vec = jnp.concatenate([bias, gain], axis=0)]
    pallas_call x2, Pallas kernels: 6.33 us -> 5.66 us  [shards(): pl.pallas_call(functools.partial(finish_kernel, rounds, final), out_shape...]
    ppermute x6, starting transfers between devices: 11.7 us -> 12.2 us  [swap(): return lax.ppermute(block, AXES[axis], route)]
    pallas_call x1, Pallas kernels: 1.29 us -> 1.77 us  [shards(): pl.pallas_call(functools.partial(pick_kernel, rounds), out_shape=[state_s...]
    ppermute x4 -> x5, starting transfers between devices: 1.13 us -> 1.59 us  [shards(): other = tuple((lax.ppermute(w, 'section', cross) for w in mine))]
  transfers between devices with their start and end apart: 10 -> 11, of which waited for: 4 -> 5; matrix products, arithmetic and copies ran while one was open for 2% -> 0% of each run, Pallas kernels for 13% -> 20%
where the time goes in v2:
time: 34.1 us; the launch traced here: 34 us
  starting transfers between devices  13.8 us (40%)
  Pallas kernels  12.4 us (36%)
  waiting for transfers between devices  7.62 us (22%)
    ppermute x6, starting transfers between devices, swap(): return lax.ppermute(block, AXES[axis], route)  12.2 us
    ppermute x6, waiting for transfers between devices, swap(): return lax.ppermute(block, AXES[axis], route)  6.41 us
    pallas_call x2, Pallas kernels, shards(): pl.pallas_call(functools.partial(finish_kernel, rounds, final), out_shape...  5.66 us
    pallas_call x2, Pallas kernels, shards(): pl.pallas_call(functools.partial(local_kernel, layer), out_shape=[wide, w...  4.95 us
    pallas_call x1, Pallas kernels, shards(): pl.pallas_call(functools.partial(pick_kernel, rounds), out_shape=[state_s...  1.77 us
    ppermute x5, starting transfers between devices, shards(): other = tuple((lax.ppermute(w, 'section', cross) for w in mine))  1.59 us
    ppermute x5, waiting for transfers between devices, shards(): other = tuple((lax.ppermute(w, 'section', cross) for w in mine))  1.21 us
  transfers between devices with their start and end apart: 11, of which 5 were waited for; matrix products, arithmetic and copies ran while one was open for 0% of the time, Pallas kernels for 20%

profile of v2, /device:TPU:0, one launch (start us, length us, event | category | flops | bytes accessed | tf_op | source)
XLA Modules:
  0.0 34.0 jit_solution(6774482348025028618)
XLA Ops:
  0.0 0.6 %collective-permute-start.1 = (bf16[1,1024,512]{2,1,0:T(8,128)(2,1)}, bf16[1,1024,512]{2,1,0:T(8,128)(2,1)S(1)}, u32[]{:S(2)}, u32[]{:S(2)}) collective-permute-start(bf16[1,1024,512]{2,1,0:T(8,128)(2,1)} %in_a.3), channel_id=1, source_target_pairs={{0,1},{1,0},{2,3},{3,2},{4,5},{5,4},{6,7},{7,6},{8,9},{9,8},{10,11... | collective-permute-start | bytes 3145736 | tf_op jit(solution)/shard_map/ppermute | solution.py:207
  0.6 0.1 collective-permute-start
  0.7 0.4 %collective-permute-start.2 = (bf16[1,512,512]{2,1,0:T(8,128)(2,1)}, bf16[1,512,512]{2,1,0:T(8,128)(2,1)S(1)}, u32[]{:S(2)}, u32[]{:S(2)}) collective-permute-start(bf16[1,512,512]{2,1,0:T(8,128)(2,1)} %out_a.3), channel_id=1, source_target_pairs={{0,1},{1,0},{2,3},{3,2},{4,5},{5,4},{6,7},{7,6},{8,9},{9,8},{10,11... | collective-permute-start | bytes 1572872 | tf_op jit(solution)/shard_map/ppermute | solution.py:207
  1.1 0.1 collective-permute-start.3
  1.2 0.4 %collective-permute-start.4 = (f32[1,512]{1,0:T(1,128)}, f32[1,512]{1,0:T(1,128)S(1)}, u32[]{:S(2)}, u32[]{:S(2)}) collective-permute-start(f32[1,512]{1,0:T(1,128)} %gain_a.3), channel_id=1, source_target_pairs={{0,1},{1,0},{2,3},{3,2},{4,5},{5,4},{6,7},{7,6},{8,9},{9,8},{10,11... | collective-permute-start | bytes 6152 | tf_op jit(solution)/shard_map/ppermute | solution.py:207
  1.6 1.8 %pick.1 = (bf16[2,384,512]{2,1,0:T(8,128)(2,1)S(1)}, bf16[2,128,512]{2,1,0:T(8,128)(2,1)S(1)}, bf16[2,128,512]{2,1,0:T(8,128)(2,1)S(1)}, bf16[2,128,512]{2,1,0:T(8,128)(2,1)S(1)}) custom-call(s32[1,4,128]{2,1,0:T(4,128)} %halo_ref.3, bf16[4,384,512]{2,1,0:T(8,128)(2,1)} %nodes_ref.1), custom_call_target="tpu_custom_call" | custom-call | flops 402653184 | bytes 1572864 | tf_op jit(solution)/shard_map/pick/pallas_call | solution.py:209
  3.4 1.2 %collective-permute-done.3.bias_b = f32[1,512]{1,0:T(1,128)S(1)} collective-permute-done((f32[1,512]{1,0:T(1,128)}, f32[1,512]{1,0:T(1,128)S(1)}, u32[]{:S(2)}, u32[]{:S(2)}) %collective-permute-start.3) | collective-permute-done | bytes 2080 | tf_op jit(solution)/shard_map/ppermute | solution.py:207
  4.6 0.7 %collective-permute-start.5 = (bf16[2,128,512]{2,1,0:T(8,128)(2,1)S(1)}, bf16[2,128,512]{2,1,0:T(8,128)(2,1)S(1)}, u32[]{:S(2)}, u32[]{:S(2)}) collective-permute-start(bf16[2,128,512]{2,1,0:T(8,128)(2,1)S(1)} %get-tuple-element.29), channel_id=1, source_target_pairs={{4,8},{8,4},{5,9},{9,5},{6,10},{10,6},{7,11},{11,7},{20,24},{24,20... | collective-permute-start | bytes 786440 | tf_op jit(solution)/shard_map/ppermute | solution.py:29
  5.3 0.0 collective-permute-done.4.gain_b
  5.3 5.8 %collective-permute-start.6 = (bf16[2,128,512]{2,1,0:T(8,128)(2,1)S(1)}, bf16[2,128,512]{2,1,0:T(8,128)(2,1)S(1)}, u32[]{:S(2)}, u32[]{:S(2)}) collective-permute-start(bf16[2,128,512]{2,1,0:T(8,128)(2,1)S(1)} %get-tuple-element.30), channel_id=1, source_target_pairs={{0,4},{4,0},{8,12},{12,8},{1,5},{5,1},{9,13},{13,9},{2,6},{6,2},{1... | collective-permute-start | bytes 786440 | tf_op jit(solution)/shard_map/ppermute | solution.py:29
  11.1 0.0 collective-permute-done.msg_b
  11.1 1.5 %collective-permute-start.7 = (bf16[2,128,512]{2,1,0:T(8,128)(2,1)S(1)}, bf16[2,128,512]{2,1,0:T(8,128)(2,1)S(1)}, u32[]{:S(2)}, u32[]{:S(2)}) collective-permute-start(bf16[2,128,512]{2,1,0:T(8,128)(2,1)S(1)} %get-tuple-element.31), channel_id=1, source_target_pairs={{0,2},{2,0},{1,3},{3,1},{4,6},{6,4},{5,7},{7,5},{8,10},{10,8},{9,1... | collective-permute-start | bytes 786440 | tf_op jit(solution)/shard_map/ppermute | solution.py:29
  12.6 0.0 collective-permute-done.2.out_b
  12.6 0.0 collective-permute-done.1.in_b
  12.6 0.0 copy-done.3
  12.6 0.0 copy-done.4
  12.6 0.0 copy-done
  12.6 0.0 copy-start.2
  12.6 3.0 %local0.1 = (f32[2,384,512]{2,1,0:T(8,128)S(1)}, f32[2,384,512]{2,1,0:T(8,128)S(1)}, bf16[512,512]{1,0:T(8,128)(2,1)S(1)}, bf16[512,512]{1,0:T(8,128)(2,1)S(1)}, f32[1,512]{1,0:T(1,128)S(1)}) custom-call(s32[3,4]{1,0:T(4,128)S(1)} %copy-done.1, bf16[3,4,128,128]{3,2,1,0:T(8,128)(2,1)S(1)} %copy-done, bf16[2,384,512]{2,1,0:T(8,128)(2,1)S(1)} %get-tuple-element.23.state_ref, ...), custom_call_target="tpu_custom_call" | custom-call | flops 1207959552 | bytes 3145728 | tf_op jit(solution)/shard_map/local0/pallas_call | solution.py:229
  15.6 0.0 collective-permute-done.5.rest_0_
  15.6 1.8 %collective-permute-done.6.rest_1_ = bf16[2,128,512]{2,1,0:T(8,128)(2,1)S(1)} collective-permute-done((bf16[2,128,512]{2,1,0:T(8,128)(2,1)S(1)}, bf16[2,128,512]{2,1,0:T(8,128)(2,1)S(1)}, u32[]{:S(2)}, u32[]{:S(2)}) %collective-permute-start.6) | collective-permute-done | bytes 262176 | tf_op jit(solution)/shard_map/ppermute | solution.py:29
  17.4 1.5 %collective-permute-done.7.rest_2_ = bf16[2,128,512]{2,1,0:T(8,128)(2,1)S(1)} collective-permute-done((bf16[2,128,512]{2,1,0:T(8,128)(2,1)S(1)}, bf16[2,128,512]{2,1,0:T(8,128)(2,1)S(1)}, u32[]{:S(2)}, u32[]{:S(2)}) %collective-permute-start.7) | collective-permute-done | bytes 262176 | tf_op jit(solution)/shard_map/ppermute | solution.py:29
  18.9 0.0 copy-done.2
  18.9 2.7 %finish0.1 = (bf16[2,384,512]{2,1,0:T(8,128)(2,1)S(1)}, bf16[2,128,512]{2,1,0:T(8,128)(2,1)S(1)}, bf16[2,128,512]{2,1,0:T(8,128)(2,1)S(1)}, bf16[2,128,512]{2,1,0:T(8,128)(2,1)S(1)}) custom-call(s32[3,4]{1,0:T(4,128)S(1)} %copy-done.1, bf16[3,4,128,128]{3,2,1,0:T(8,128)(2,1)S(1)} %copy-done, s32[1,4,128]{2,1,0:T(4,128)S(1)} %copy-done.2, ...), custom_call_target="tpu_custom_call" | custom-call | flops 1207959552 | bytes 3145728 | tf_op jit(solution)/shard_map/finish0/pallas_call | solution.py:243
  21.5 0.7 %collective-permute-start.8 = (bf16[2,128,512]{2,1,0:T(8,128)(2,1)S(1)}, bf16[2,128,512]{2,1,0:T(8,128)(2,1)S(1)}, u32[]{:S(2)}, u32[]{:S(2)}) collective-permute-start(bf16[2,128,512]{2,1,0:T(8,128)(2,1)S(1)} %get-tuple-element.38), channel_id=1, source_target_pairs={{4,8},{8,4},{5,9},{9,5},{6,10},{10,6},{7,11},{11,7},{20,24},{24,20... | collective-permute-start | bytes 786440 | tf_op jit(solution)/shard_map/ppermute | solution.py:29
  22.2 2.1 %collective-permute-start.9 = (bf16[2,128,512]{2,1,0:T(8,128)(2,1)S(1)}, bf16[2,128,512]{2,1,0:T(8,128)(2,1)S(1)}, u32[]{:S(2)}, u32[]{:S(2)}) collective-permute-start(bf16[2,128,512]{2,1,0:T(8,128)(2,1)S(1)} %get-tuple-element.39), channel_id=1, source_target_pairs={{0,4},{4,0},{8,12},{12,8},{1,5},{5,1},{9,13},{13,9},{2,6},{6,2},{1... | collective-permute-start | bytes 786440 | tf_op jit(solution)/shard_map/ppermute | solution.py:29
  24.3 1.5 %collective-permute-start.10 = (bf16[2,128,512]{2,1,0:T(8,128)(2,1)S(1)}, bf16[2,128,512]{2,1,0:T(8,128)(2,1)S(1)}, u32[]{:S(2)}, u32[]{:S(2)}) collective-permute-start(bf16[2,128,512]{2,1,0:T(8,128)(2,1)S(1)} %get-tuple-element.40), channel_id=1, source_target_pairs={{0,2},{2,0},{1,3},{3,1},{4,6},{6,4},{5,7},{7,5},{8,10},{10,8},{9,1... | collective-permute-start | bytes 786440 | tf_op jit(solution)/shard_map/ppermute | solution.py:29
  25.8 2.0 %local1.1 = (f32[2,384,512]{2,1,0:T(8,128)S(1)}, f32[2,384,512]{2,1,0:T(8,128)S(1)}, bf16[512,512]{1,0:T(8,128)(2,1)S(1)}, bf16[512,512]{1,0:T(8,128)(2,1)S(1)}, f32[1,512]{1,0:T(1,128)S(1)}) custom-call(s32[3,4]{1,0:T(4,128)S(1)} %copy-done.1, bf16[3,4,128,128]{3,2,1,0:T(8,128)(2,1)S(1)} %copy-done, bf16[2,384,512]{2,1,0:T(8,128)(2,1)S(1)} %get-tuple-element.32.state_ref, ...), custom_call_target="tpu_custom_call" | custom-call | flops 1207959552 | bytes 3145728 | tf_op jit(solution)/shard_map/local1/pallas_call | solution.py:229
  27.8 0.0 collective-permute-done.8.rest_0_
  27.8 1.7 %collective-permute-done.9.rest_1_ = bf16[2,128,512]{2,1,0:T(8,128)(2,1)S(1)} collective-permute-done((bf16[2,128,512]{2,1,0:T(8,128)(2,1)S(1)}, bf16[2,128,512]{2,1,0:T(8,128)(2,1)S(1)}, u32[]{:S(2)}, u32[]{:S(2)}) %collective-permute-start.9) | collective-permute-done | bytes 262176 | tf_op jit(solution)/shard_map/ppermute | solution.py:29
  29.5 1.5 %collective-permute-done.10.rest_2_ = bf16[2,128,512]{2,1,0:T(8,128)(2,1)S(1)} collective-permute-done((bf16[2,128,512]{2,1,0:T(8,128)(2,1)S(1)}, bf16[2,128,512]{2,1,0:T(8,128)(2,1)S(1)}, u32[]{:S(2)}, u32[]{:S(2)}) %collective-permute-start.10) | collective-permute-done | bytes 262176 | tf_op jit(solution)/shard_map/ppermute | solution.py:29
  31.0 3.0 %finish1.1 = bf16[2,384,512]{2,1,0:T(8,128)(2,1)} custom-call(s32[3,4]{1,0:T(4,128)S(1)} %copy-done.1, bf16[3,4,128,128]{3,2,1,0:T(8,128)(2,1)S(1)} %copy-done, s32[1,4,128]{2,1,0:T(4,128)S(1)} %copy-done.2, bf16[2,384,512]{2,1,0:T(8,128)(2,1)S(1)} %get-tuple-element.32.state_ref, f32[2,384,512]{2,1,0:T(8,128)S(1)} %get-tuple-element.33.base_ref, ...), custom_call_target="tpu_custom_call" | custom-call | flops 1207959552 | bytes 3145728 | tf_op jit(solution)/shard_map/finish1/pallas_call | solution.py:243
  (5 shorter events, 0.0 us)
Async XLA Ops:
  0.0 12.6 %copy-start.3 = (f32[1,512]{1,0:T(1,128)S(1)}, f32[1,512]{1,0:T(1,128)}, u32[]{:S(2)}) copy-start(f32[1,512]{1,0:T(1,128)} %bias_a.3) | copy-start | bytes 6148
  0.0 12.6 %copy-start.4 = (f32[1,512]{1,0:T(1,128)S(1)}, f32[1,512]{1,0:T(1,128)}, u32[]{:S(2)}) copy-start(f32[1,512]{1,0:T(1,128)} %gain_a.3) | copy-start | bytes 6148
  0.0 12.6 %copy-start = (bf16[3,4,128,128]{3,2,1,0:T(8,128)(2,1)S(1)}, bf16[3,4,128,128]{3,2,1,0:T(8,128)(2,1)}, u32[]{:S(2)}) copy-start(bf16[3,4,128,128]{3,2,1,0:T(8,128)(2,1)} %values_ref.7) | copy-start | bytes 1179652
  0.0 12.6 %copy-start.1 = (s32[3,4]{1,0:T(4,128)S(1)}, s32[3,4]{1,0:T(4,128)}, u32[]{:S(2)}) copy-start(s32[3,4]{1,0:T(4,128)} %index_ref.7) | copy-start | bytes 148
  0.0 12.6 %collective-permute-start.1 = (bf16[1,1024,512]{2,1,0:T(8,128)(2,1)}, bf16[1,1024,512]{2,1,0:T(8,128)(2,1)S(1)}, u32[]{:S(2)}, u32[]{:S(2)}) collective-permute-start(bf16[1,1024,512]{2,1,0:T(8,128)(2,1)} %in_a.3), channel_id=1, source_target_pairs={{0,1},{1,0},{2,3},{3,2},{4,5},{5,4},{6,7},{7,6},{8,9},{9,8},{10,11... | collective-permute-start | bytes 3145736 | tf_op jit(solution)/shard_map/ppermute | solution.py:207
  0.6 10.5 %collective-permute-start = (bf16[1,512,512]{2,1,0:T(8,128)(2,1)}, bf16[1,512,512]{2,1,0:T(8,128)(2,1)S(1)}, u32[]{:S(2)}, u32[]{:S(2)}) collective-permute-start(bf16[1,512,512]{2,1,0:T(8,128)(2,1)} %msg_a.3), channel_id=1, source_target_pairs={{0,1},{1,0},{2,3},{3,2},{4,5},{5,4},{6,7},{7,6},{8,9},{9,8},{10,11... | collective-permute-start | bytes 1572872 | tf_op jit(solution)/shard_map/ppermute | solution.py:207
  0.7 11.9 %collective-permute-start.2 = (bf16[1,512,512]{2,1,0:T(8,128)(2,1)}, bf16[1,512,512]{2,1,0:T(8,128)(2,1)S(1)}, u32[]{:S(2)}, u32[]{:S(2)}) collective-permute-start(bf16[1,512,512]{2,1,0:T(8,128)(2,1)} %out_a.3), channel_id=1, source_target_pairs={{0,1},{1,0},{2,3},{3,2},{4,5},{5,4},{6,7},{7,6},{8,9},{9,8},{10,11... | collective-permute-start | bytes 1572872 | tf_op jit(solution)/shard_map/ppermute | solution.py:207
  1.1 3.5 %collective-permute-start.3 = (f32[1,512]{1,0:T(1,128)}, f32[1,512]{1,0:T(1,128)S(1)}, u32[]{:S(2)}, u32[]{:S(2)}) collective-permute-start(f32[1,512]{1,0:T(1,128)} %bias_a.3), channel_id=1, source_target_pairs={{0,1},{1,0},{2,3},{3,2},{4,5},{5,4},{6,7},{7,6},{8,9},{9,8},{10,11... | collective-permute-start | bytes 6152 | tf_op jit(solution)/shard_map/ppermute | solution.py:207
  1.2 4.1 %collective-permute-start.4 = (f32[1,512]{1,0:T(1,128)}, f32[1,512]{1,0:T(1,128)S(1)}, u32[]{:S(2)}, u32[]{:S(2)}) collective-permute-start(f32[1,512]{1,0:T(1,128)} %gain_a.3), channel_id=1, source_target_pairs={{0,1},{1,0},{2,3},{3,2},{4,5},{5,4},{6,7},{7,6},{8,9},{9,8},{10,11... | collective-permute-start | bytes 6152 | tf_op jit(solution)/shard_map/ppermute | solution.py:207
  4.6 11.0 %collective-permute-start.5 = (bf16[2,128,512]{2,1,0:T(8,128)(2,1)S(1)}, bf16[2,128,512]{2,1,0:T(8,128)(2,1)S(1)}, u32[]{:S(2)}, u32[]{:S(2)}) collective-permute-start(bf16[2,128,512]{2,1,0:T(8,128)(2,1)S(1)} %get-tuple-element.29), channel_id=1, source_target_pairs={{4,8},{8,4},{5,9},{9,5},{6,10},{10,6},{7,11},{11,7},{20,24},{24,20... | collective-permute-start | bytes 786440 | tf_op jit(solution)/shard_map/ppermute | solution.py:29
  5.3 12.1 %collective-permute-start.6 = (bf16[2,128,512]{2,1,0:T(8,128)(2,1)S(1)}, bf16[2,128,512]{2,1,0:T(8,128)(2,1)S(1)}, u32[]{:S(2)}, u32[]{:S(2)}) collective-permute-start(bf16[2,128,512]{2,1,0:T(8,128)(2,1)S(1)} %get-tuple-element.30), channel_id=1, source_target_pairs={{0,4},{4,0},{8,12},{12,8},{1,5},{5,1},{9,13},{13,9},{2,6},{6,2},{1... | collective-permute-start | bytes 786440 | tf_op jit(solution)/shard_map/ppermute | solution.py:29
  11.1 7.8 %collective-permute-start.7 = (bf16[2,128,512]{2,1,0:T(8,128)(2,1)S(1)}, bf16[2,128,512]{2,1,0:T(8,128)(2,1)S(1)}, u32[]{:S(2)}, u32[]{:S(2)}) collective-permute-start(bf16[2,128,512]{2,1,0:T(8,128)(2,1)S(1)} %get-tuple-element.31), channel_id=1, source_target_pairs={{0,2},{2,0},{1,3},{3,1},{4,6},{6,4},{5,7},{7,5},{8,10},{10,8},{9,1... | collective-permute-start | bytes 786440 | tf_op jit(solution)/shard_map/ppermute | solution.py:29
  12.6 6.3 %copy-start.2 = (s32[1,4,128]{2,1,0:T(4,128)S(1)}, s32[1,4,128]{2,1,0:T(4,128)}, u32[]{:S(2)}) copy-start(s32[1,4,128]{2,1,0:T(4,128)} %halo_ref.3) | copy-start | bytes 6148
  21.5 6.3 %collective-permute-start.8 = (bf16[2,128,512]{2,1,0:T(8,128)(2,1)S(1)}, bf16[2,128,512]{2,1,0:T(8,128)(2,1)S(1)}, u32[]{:S(2)}, u32[]{:S(2)}) collective-permute-start(bf16[2,128,512]{2,1,0:T(8,128)(2,1)S(1)} %get-tuple-element.38), channel_id=1, source_target_pairs={{4,8},{8,4},{5,9},{9,5},{6,10},{10,6},{7,11},{11,7},{20,24},{24,20... | collective-permute-start | bytes 786440 | tf_op jit(solution)/shard_map/ppermute | solution.py:29
  22.2 7.3 %collective-permute-start.9 = (bf16[2,128,512]{2,1,0:T(8,128)(2,1)S(1)}, bf16[2,128,512]{2,1,0:T(8,128)(2,1)S(1)}, u32[]{:S(2)}, u32[]{:S(2)}) collective-permute-start(bf16[2,128,512]{2,1,0:T(8,128)(2,1)S(1)} %get-tuple-element.39), channel_id=1, source_target_pairs={{0,4},{4,0},{8,12},{12,8},{1,5},{5,1},{9,13},{13,9},{2,6},{6,2},{1... | collective-permute-start | bytes 786440 | tf_op jit(solution)/shard_map/ppermute | solution.py:29
  24.3 6.6 %collective-permute-start.10 = (bf16[2,128,512]{2,1,0:T(8,128)(2,1)S(1)}, bf16[2,128,512]{2,1,0:T(8,128)(2,1)S(1)}, u32[]{:S(2)}, u32[]{:S(2)}) collective-permute-start(bf16[2,128,512]{2,1,0:T(8,128)(2,1)S(1)} %get-tuple-element.40), channel_id=1, source_target_pairs={{0,2},{2,0},{1,3},{3,1},{4,6},{6,4},{5,7},{7,5},{8,10},{10,8},{9,1... | collective-permute-start | bytes 786440 | tf_op jit(solution)/shard_map/ppermute | solution.py:29

commit v3 on v2

--- a/solution.py
+++ b/solution.py
@@ -18,15 +18,19 @@
 
 
 def meetings(sizes):
-    return [(axis, turn) for axis in range(2) for turn in (1, 0) if sizes[axis] > 1 + turn]
+    return [(axis, turn) for turn in range(2) for axis in (1, 0) if sizes[axis] > 1 + turn]
 
 
 def swap(block, axis, turn):
-    size = lax.axis_size(AXES[axis])
+    names = (AXES[axis], "section")
+    size, cores = lax.axis_size(names[0]), lax.axis_size(names[1])
     route = []
-    for low in range(turn, size - 1, 2):
-        route += [(low, low + 1), (low + 1, low)]
-    return lax.ppermute(block, AXES[axis], route)
+    for at in range(size):
+        partner = at + 1 if (at + turn) % 2 == 0 else at - 1
+        for core in range(cores):
+            there = (partner, core) if 0 <= partner < size else (at, cores - 1 - core)
+            route.append((at * cores + core, there[0] * cores + there[1]))
+    return lax.ppermute(block, names, route)
 
 
 def select_rows(halo_ref, rounds, rows):
@@ -50,9 +54,9 @@
     )
 
 
-def pick_kernel(rounds, halo_hbm, nodes_ref, state_ref, *rest):
+def pick_kernel(rounds, halo_hbm, nodes_ref, bias_hbm, gain_hbm, state_ref, vec_ref, *rest):
     sends, (halo_ref, sem) = rest[: len(rounds)], rest[len(rounds) :]
-    half, rows, _ = state_ref.shape
+    half, rows, width = state_ref.shape
     section = lax.axis_index("section")
     lists = pltpu.make_async_copy(halo_hbm, halo_ref, sem.at[half])
     lists.start()
@@ -62,6 +66,12 @@
     ]
     for copy in fetch:
         copy.start()
+    lines = [
+        pltpu.make_async_copy(line, vec_ref.at[:, pl.ds(n * width, width)], sem.at[half + 1 + n])
+        for n, line in enumerate((bias_hbm, gain_hbm))
+    ]
+    for copy in lines:
+        copy.start()
     lists.wait()
     chosen = select_rows(halo_ref, rounds, rows)
     count = chosen.shape[0] // len(rounds)
@@ -70,11 +80,13 @@
         sent = dot(chosen, state_ref[b]).astype(BF16)
         for n, ref in enumerate(sends):
             ref[b] = sent[n * count : (n + 1) * count]
+    for copy in lines:
+        copy.wait()
 
 
 def local_kernel(
     layer, index_ref, values_ref, state_ref,
-    msg_a, msg_b, in_a, in_b, out_a, out_b, bias_a, bias_b, gain_a, gain_b,
+    msg_a, msg_b, in_a, in_b, out_a, out_b, vec_a, vec_b,
     base_ref, near_ref, fold_ref, last_ref, gain_ref, msg_ref, in_ref, sem,
 ):
     mine = lax.axis_index("section") == layer
@@ -101,8 +113,9 @@
         for copy in came:
             copy.start()
 
-    gain_ref[...] = jnp.where(mine, gain_a[...], gain_b[...])
-    bias = jnp.where(mine, bias_a[...], bias_b[...])
+    vec = jnp.where(mine, vec_a[...], vec_b[...])
+    bias = vec[:, :width]
+    gain_ref[...] = vec[:, width:]
     for r in range(tiles):
         other = pl.multiple_of(index_ref[r, 1] * tile, tile)
         edges = jnp.concatenate([values_ref[r, 0], values_ref[r, 1]], axis=1)
@@ -129,23 +142,24 @@
     ext, rest = rest[0], rest[1:]
     half, rows, width = base_ref.shape
     tiles, _, tile, _ = values_ref.shape
-    for slot in range(4):
-        here = (slot // 2, slot % 2)
-        if here in rounds:
-            ext[slot] = recvs[rounds.index(here)][...]
-        else:
-            ext[slot] = jnp.zeros(ext.shape[1:], BF16)
+    for (axis, turn), recv in zip(rounds, recvs):
+        ext[2 * axis + turn] = recv[...]
+    ext[4] = jnp.zeros(ext.shape[1:], BF16)
 
     def slot_of(entry):
         place = entry - tiles
         axis, upper = lax.div(place, 2), lax.rem(place, 2)
-        at = jnp.where(axis == 0, lax.axis_index("slabx"), lax.axis_index("slaby"))
-        return 2 * axis + 1 - lax.rem(upper + at, 2)
+        first = axis == 0
+        at = jnp.where(first, lax.axis_index(AXES[0]), lax.axis_index(AXES[1]))
+        size = jnp.where(first, lax.axis_size(AXES[0]), lax.axis_size(AXES[1]))
+        exists = jnp.where(upper == 1, at + 1 < size, at > 0)
+        return jnp.where(exists, 2 * axis + 1 - lax.rem(upper + at, 2), 4)
 
     slots = [[slot_of(index_ref[r, 2]), slot_of(index_ref[r, 3])] for r in range(tiles)]
     gain = gain_ref[...]
-    acts, outs = [], []
-    for b in range(half):
+    writes = []
+
+    def project(b):
         parts = []
         for r in range(tiles):
             pair = jnp.concatenate([ext[slots[r][0], b], ext[slots[r][1], b]], axis=0)
@@ -154,13 +168,9 @@
             parts.append(far.astype(BF16))
         total = jnp.concatenate(parts, axis=0)
         pre = base_ref[b] + dot(total, fold_ref[...])
-        acts.append(jnp.maximum(pre, 0.0).astype(BF16))
-    for b in range(half):
-        outs.append(dot(acts[b], last_ref[...]))
-    chosen = None if final else select_rows(halo_ref, rounds, rows)
-    writes = []
-    for b in range(half):
-        out = outs[b]
+        return dot(jnp.maximum(pre, 0.0).astype(BF16), last_ref[...])
+
+    def settle(b, out):
         mean = jnp.mean(out, axis=-1, keepdims=True)
         off = out - mean
         var = jnp.mean(off * off, axis=-1, keepdims=True)
@@ -173,9 +183,21 @@
             writes[b].start()
         else:
             out_ref[b] = fresh
-            sent = dot(chosen, fresh).astype(BF16)
-            for n, ref in enumerate(sends):
-                ref[b] = sent[n * tile : (n + 1) * tile]
+        return fresh
+
+    def send(b, fresh):
+        sent = dot(chosen, fresh).astype(BF16)
+        for n, ref in enumerate(sends):
+            ref[b] = sent[n * tile : (n + 1) * tile]
+
+    chosen = None if final else select_rows(halo_ref, rounds, rows)
+    outs = [project(0)]
+    for b in range(half):
+        if b + 1 < half:
+            outs.append(project(b + 1))
+        fresh = settle(b, outs[b])
+        if not final:
+            send(b, fresh)
     for copy in writes:
         copy.wait()
 
@@ -196,40 +218,44 @@
     wide = jax.ShapeDtypeStruct((half, rows, width), F32)
     square = jax.ShapeDtypeStruct((width, width), BF16)
     line = jax.ShapeDtypeStruct((1, width), F32)
+    vec_shape = jax.ShapeDtypeStruct((1, 2 * width), F32)
 
     def cost(matmul_rows, nbytes):
         return pl.CostEstimate(
             flops=2 * matmul_rows * width * width, bytes_accessed=nbytes, transcendentals=0
         )
 
-    mine = (w_msg, w_in, w_out, bias, gain)
+    mine = (w_msg, w_in, w_out)
     cross = [(0, 1), (1, 0)]
+    in_hbm = lambda a: pltpu.with_memory_space_constraint(a, pltpu.HBM)
     other = tuple(lax.ppermute(w, "section", cross) for w in mine)
 
-    state, *sends = pl.pallas_call(
+    state, vec, *sends = pl.pallas_call(
         functools.partial(pick_kernel, rounds),
-        out_shape=[state_shape] + [block] * len(rounds),
-        in_specs=[HBM, HBM],
-        out_specs=[VMEM] * (1 + len(rounds)),
+        out_shape=[state_shape, vec_shape] + [block] * len(rounds),
+        in_specs=[HBM] * 4,
+        out_specs=[VMEM] * (2 + len(rounds)),
         scratch_shapes=[
             pltpu.VMEM(halo_rows.shape, jnp.int32),
-            pltpu.SemaphoreType.DMA((half + 1,)),
+            pltpu.SemaphoreType.DMA((half + 3,)),
         ],
         cost_estimate=cost(half * rows, 2 * half * rows * width * 2),
         compiler_params=pltpu.CompilerParams(vmem_limit_bytes=LIMIT),
         name="pick",
-    )(pltpu.with_memory_space_constraint(halo_rows, pltpu.HBM), pltpu.with_memory_space_constraint(nodes, pltpu.HBM))
+    )(*(in_hbm(a) for a in (halo_rows, nodes, bias, gain)))
+    swapped = lax.ppermute(vec, "section", cross)
 
     for layer in range(2):
         final = layer == 1
         got = [swap(sent, *turn) for sent, turn in zip(sends, rounds)]
         weights = []
-        for n, (a, b) in enumerate(zip(mine, other)):
-            weights += [pltpu.with_memory_space_constraint(a, pltpu.HBM) if n < 3 else a, b]
+        for a, b in zip(mine, other):
+            weights += [in_hbm(a), b]
+        weights += [vec, swapped]
         base, near, fold, last, line_gain = pl.pallas_call(
             functools.partial(local_kernel, layer),
             out_shape=[wide, wide, square, square, line],
-            in_specs=[SMEM] + [VMEM] * 2 + [HBM, VMEM] * 3 + [VMEM] * 4,
+            in_specs=[SMEM] + [VMEM] * 2 + [HBM, VMEM] * 3 + [VMEM] * 2,
             out_specs=[VMEM] * 5,
             scratch_shapes=[
                 pltpu.VMEM((width, width), BF16),
@@ -245,7 +271,7 @@
             out_shape=[state_shape] + ([] if final else [block] * len(rounds)),
             in_specs=[SMEM] + [VMEM] * (8 + len(rounds)),
             out_specs=[HBM] if final else [VMEM] * (1 + len(rounds)),
-            scratch_shapes=[pltpu.VMEM((4, half, tile, width), BF16)]
+            scratch_shapes=[pltpu.VMEM((5, half, tile, width), BF16)]
             + (
                 [pltpu.VMEM((half, rows, width), BF16), pltpu.SemaphoreType.DMA((half,))]
                 if final

time: 34.1 us -> 29.8 us (0.87)
  starting transfers between devices: 13.8 us -> 10.1 us
  waiting for transfers between devices: 7.62 us -> 7.05 us
    ppermute x6 -> x7, starting transfers between devices: 12.2 us -> 9.06 us  [the longest x6 8.92 us: swap(): return lax.ppermute(block, names, route)]
    ppermute x5 -> x3, waiting for transfers between devices: 1.21 us -> 0.01 us  [shards(): other = tuple((lax.ppermute(w, 'section', cross) for w in mine))]
    ppermute x6 -> x7, waiting for transfers between devices: 6.41 us -> 7.05 us  [the longest x6 7.04 us: swap(): return lax.ppermute(block, names, route)]
    ppermute x5 -> x3, starting transfers between devices: 1.59 us -> 1 us  [shards(): other = tuple((lax.ppermute(w, 'section', cross) for w in mine))]
  transfers between devices with their start and end apart: 11 -> 10, of which waited for: 5 -> 4; matrix products, arithmetic and copies ran while one was open for 0% -> 0% of each run, Pallas kernels for 20% -> 23%
where the time goes in v3:
time: 29.8 us; the launch traced here: 29.7 us
  Pallas kernels  12.5 us (42%)
  starting transfers between devices  10.1 us (34%)
  waiting for transfers between devices  7.05 us (24%)
    ppermute x6, starting transfers between devices, swap(): return lax.ppermute(block, names, route)  8.92 us
    ppermute x6, waiting for transfers between devices, swap(): return lax.ppermute(block, names, route)  7.04 us
    pallas_call x2, Pallas kernels, shards(): pl.pallas_call(functools.partial(finish_kernel, rounds, final), out_shape...  5.72 us
    pallas_call x2, Pallas kernels, shards(): pl.pallas_call(functools.partial(local_kernel, layer), out_shape=[wide, w...  4.95 us
    pallas_call x1, Pallas kernels, shards(): pl.pallas_call(functools.partial(pick_kernel, rounds), out_shape=[state_s...  1.8 us
    ppermute x3, starting transfers between devices, shards(): other = tuple((lax.ppermute(w, 'section', cross) for w in mine))  1 us
  transfers between devices with their start and end apart: 10, of which 4 were waited for; matrix products, arithmetic and copies ran while one was open for 0% of the time, Pallas kernels for 23%

profile of v3, /device:TPU:0, one launch (start us, length us, event | category | flops | bytes accessed | tf_op | source)
XLA Modules:
  0.0 29.7 jit_solution(10257824836198844846)
XLA Ops:
  0.0 0.0 copy-start
  0.0 0.0 copy-start.1
  0.0 0.5 %collective-permute-start.1 = (bf16[1,1024,512]{2,1,0:T(8,128)(2,1)}, bf16[1,1024,512]{2,1,0:T(8,128)(2,1)S(1)}, u32[]{:S(2)}, u32[]{:S(2)}) collective-permute-start(bf16[1,1024,512]{2,1,0:T(8,128)(2,1)} %in_a.3), channel_id=1, source_target_pairs={{0,1},{1,0},{2,3},{3,2},{4,5},{5,4},{6,7},{7,6},{8,9},{9,8},{10,11... | collective-permute-start | bytes 3145736 | tf_op jit(solution)/shard_map/ppermute | solution.py:231
  0.5 0.1 collective-permute-start
  0.6 0.4 %collective-permute-start.2 = (bf16[1,512,512]{2,1,0:T(8,128)(2,1)}, bf16[1,512,512]{2,1,0:T(8,128)(2,1)S(1)}, u32[]{:S(2)}, u32[]{:S(2)}) collective-permute-start(bf16[1,512,512]{2,1,0:T(8,128)(2,1)} %out_a.3), channel_id=1, source_target_pairs={{0,1},{1,0},{2,3},{3,2},{4,5},{5,4},{6,7},{7,6},{8,9},{9,8},{10,11... | collective-permute-start | bytes 1572872 | tf_op jit(solution)/shard_map/ppermute | solution.py:231
  1.0 1.8 %pick.1 = (bf16[2,384,512]{2,1,0:T(8,128)(2,1)S(1)}, f32[1,1024]{1,0:T(1,128)S(1)}, bf16[2,128,512]{2,1,0:T(8,128)(2,1)S(1)}, bf16[2,128,512]{2,1,0:T(8,128)(2,1)S(1)}, bf16[2,128,512]{2,1,0:T(8,128)(2,1)S(1)}) custom-call(s32[1,4,128]{2,1,0:T(4,128)} %halo_ref.3, bf16[4,384,512]{2,1,0:T(8,128)(2,1)} %nodes_ref.1, f32[1,512]{1,0:T(1,128)} %bias_hbm.1, ...), custom_call_target="tpu_custom_call" | custom-call | flops 402653184 | bytes 1572864 | tf_op jit(solution)/shard_map/pick/pallas_call | solution.py:233
  2.8 0.1 collective-permute-start.3
  3.0 2.9 %collective-permute-start.4 = (bf16[2,128,512]{2,1,0:T(8,128)(2,1)S(1)}, bf16[2,128,512]{2,1,0:T(8,128)(2,1)S(1)}, u32[]{:S(2)}, u32[]{:S(2)}) collective-permute-start(bf16[2,128,512]{2,1,0:T(8,128)(2,1)S(1)} %get-tuple-element.31), channel_id=1, source_target_pairs={{0,2},{1,3},{2,0},{3,1},{4,6},{5,7},{6,4},{7,5},{8,10},{9,11},{10,... | collective-permute-start | bytes 786440 | tf_op jit(solution)/shard_map/ppermute | solution.py:33
  5.9 0.0 collective-permute-done.3.vec_b
  5.9 1.6 %collective-permute-start.5 = (bf16[2,128,512]{2,1,0:T(8,128)(2,1)S(1)}, bf16[2,128,512]{2,1,0:T(8,128)(2,1)S(1)}, u32[]{:S(2)}, u32[]{:S(2)}) collective-permute-start(bf16[2,128,512]{2,1,0:T(8,128)(2,1)S(1)} %get-tuple-element.32), channel_id=1, source_target_pairs={{0,4},{1,5},{4,0},{5,1},{8,12},{9,13},{12,8},{13,9},{2,6},{3,7},{6... | collective-permute-start | bytes 786440 | tf_op jit(solution)/shard_map/ppermute | solution.py:33
  7.4 0.0 collective-permute-done.msg_b
  7.4 0.0 collective-permute-start.6
  7.5 0.0 collective-permute-done.2.out_b
  7.5 0.0 collective-permute-done.1.in_b
  7.5 0.0 copy-done
  7.5 0.0 copy-done.1
  7.5 0.0 copy-start.2
  7.5 3.0 %local0.1 = (f32[2,384,512]{2,1,0:T(8,128)S(1)}, f32[2,384,512]{2,1,0:T(8,128)S(1)}, bf16[512,512]{1,0:T(8,128)(2,1)S(1)}, bf16[512,512]{1,0:T(8,128)(2,1)S(1)}, f32[1,512]{1,0:T(1,128)S(1)}) custom-call(s32[3,4]{1,0:T(4,128)S(1)} %copy-done.1, bf16[3,4,128,128]{3,2,1,0:T(8,128)(2,1)S(1)} %copy-done, bf16[2,384,512]{2,1,0:T(8,128)(2,1)S(1)} %get-tuple-element.24.state_ref, ...), custom_call_target="tpu_custom_call" | custom-call | flops 1207959552 | bytes 3145728 | tf_op jit(solution)/shard_map/local0/pallas_call | solution.py:255
  10.5 1.9 %collective-permute-done.4.rest_0_ = bf16[2,128,512]{2,1,0:T(8,128)(2,1)S(1)} collective-permute-done((bf16[2,128,512]{2,1,0:T(8,128)(2,1)S(1)}, bf16[2,128,512]{2,1,0:T(8,128)(2,1)S(1)}, u32[]{:S(2)}, u32[]{:S(2)}) %collective-permute-start.4) | collective-permute-done | bytes 262176 | tf_op jit(solution)/shard_map/ppermute | solution.py:33
  12.4 1.6 %collective-permute-done.5.rest_1_ = bf16[2,128,512]{2,1,0:T(8,128)(2,1)S(1)} collective-permute-done((bf16[2,128,512]{2,1,0:T(8,128)(2,1)S(1)}, bf16[2,128,512]{2,1,0:T(8,128)(2,1)S(1)}, u32[]{:S(2)}, u32[]{:S(2)}) %collective-permute-start.5) | collective-permute-done | bytes 262176 | tf_op jit(solution)/shard_map/ppermute | solution.py:33
  14.0 0.0 collective-permute-done.6.rest_2_
  14.0 0.0 copy-done.2
  14.0 2.6 %finish0.1 = (bf16[2,384,512]{2,1,0:T(8,128)(2,1)S(1)}, bf16[2,128,512]{2,1,0:T(8,128)(2,1)S(1)}, bf16[2,128,512]{2,1,0:T(8,128)(2,1)S(1)}, bf16[2,128,512]{2,1,0:T(8,128)(2,1)S(1)}) custom-call(s32[3,4]{1,0:T(4,128)S(1)} %copy-done.1, bf16[3,4,128,128]{3,2,1,0:T(8,128)(2,1)S(1)} %copy-done, s32[1,4,128]{2,1,0:T(4,128)S(1)} %copy-done.2, ...), custom_call_target="tpu_custom_call" | custom-call | flops 1207959552 | bytes 3145728 | tf_op jit(solution)/shard_map/finish0/pallas_call | solution.py:269
  16.7 1.7 %collective-permute-start.7 = (bf16[2,128,512]{2,1,0:T(8,128)(2,1)S(1)}, bf16[2,128,512]{2,1,0:T(8,128)(2,1)S(1)}, u32[]{:S(2)}, u32[]{:S(2)}) collective-permute-start(bf16[2,128,512]{2,1,0:T(8,128)(2,1)S(1)} %get-tuple-element.40), channel_id=1, source_target_pairs={{0,2},{1,3},{2,0},{3,1},{4,6},{5,7},{6,4},{7,5},{8,10},{9,11},{10,... | collective-permute-start | bytes 786440 | tf_op jit(solution)/shard_map/ppermute | solution.py:33
  18.4 2.7 %collective-permute-start.8 = (bf16[2,128,512]{2,1,0:T(8,128)(2,1)S(1)}, bf16[2,128,512]{2,1,0:T(8,128)(2,1)S(1)}, u32[]{:S(2)}, u32[]{:S(2)}) collective-permute-start(bf16[2,128,512]{2,1,0:T(8,128)(2,1)S(1)} %get-tuple-element.41), channel_id=1, source_target_pairs={{0,4},{1,5},{4,0},{5,1},{8,12},{9,13},{12,8},{13,9},{2,6},{3,7},{6... | collective-permute-start | bytes 786440 | tf_op jit(solution)/shard_map/ppermute | solution.py:33
  21.1 0.0 collective-permute-start.9
  21.1 2.0 %local1.1 = (f32[2,384,512]{2,1,0:T(8,128)S(1)}, f32[2,384,512]{2,1,0:T(8,128)S(1)}, bf16[512,512]{1,0:T(8,128)(2,1)S(1)}, bf16[512,512]{1,0:T(8,128)(2,1)S(1)}, f32[1,512]{1,0:T(1,128)S(1)}) custom-call(s32[3,4]{1,0:T(4,128)S(1)} %copy-done.1, bf16[3,4,128,128]{3,2,1,0:T(8,128)(2,1)S(1)} %copy-done, bf16[2,384,512]{2,1,0:T(8,128)(2,1)S(1)} %get-tuple-element.34.state_ref, ...), custom_call_target="tpu_custom_call" | custom-call | flops 1207959552 | bytes 3145728 | tf_op jit(solution)/shard_map/local1/pallas_call | solution.py:255
  23.1 1.1 %collective-permute-done.7.rest_0_ = bf16[2,128,512]{2,1,0:T(8,128)(2,1)S(1)} collective-permute-done((bf16[2,128,512]{2,1,0:T(8,128)(2,1)S(1)}, bf16[2,128,512]{2,1,0:T(8,128)(2,1)S(1)}, u32[]{:S(2)}, u32[]{:S(2)}) %collective-permute-start.7) | collective-permute-done | bytes 262176 | tf_op jit(solution)/shard_map/ppermute | solution.py:33
  24.1 2.4 %collective-permute-done.8.rest_1_ = bf16[2,128,512]{2,1,0:T(8,128)(2,1)S(1)} collective-permute-done((bf16[2,128,512]{2,1,0:T(8,128)(2,1)S(1)}, bf16[2,128,512]{2,1,0:T(8,128)(2,1)S(1)}, u32[]{:S(2)}, u32[]{:S(2)}) %collective-permute-start.8) | collective-permute-done | bytes 262176 | tf_op jit(solution)/shard_map/ppermute | solution.py:33
  26.6 0.0 collective-permute-done.9.rest_2_
  26.6 3.1 %finish1.1 = bf16[2,384,512]{2,1,0:T(8,128)(2,1)} custom-call(s32[3,4]{1,0:T(4,128)S(1)} %copy-done.1, bf16[3,4,128,128]{3,2,1,0:T(8,128)(2,1)S(1)} %copy-done, s32[1,4,128]{2,1,0:T(4,128)S(1)} %copy-done.2, bf16[2,384,512]{2,1,0:T(8,128)(2,1)S(1)} %get-tuple-element.34.state_ref, f32[2,384,512]{2,1,0:T(8,128)S(1)} %get-tuple-element.35.base_ref, ...), custom_call_target="tpu_custom_call" | custom-call | flops 1207959552 | bytes 3145728 | tf_op jit(solution)/shard_map/finish1/pallas_call | solution.py:269
Async XLA Ops:
  0.0 7.5 %copy-start = (bf16[3,4,128,128]{3,2,1,0:T(8,128)(2,1)S(1)}, bf16[3,4,128,128]{3,2,1,0:T(8,128)(2,1)}, u32[]{:S(2)}) copy-start(bf16[3,4,128,128]{3,2,1,0:T(8,128)(2,1)} %values_ref.7) | copy-start | bytes 1179652
  0.0 7.5 %copy-start.1 = (s32[3,4]{1,0:T(4,128)S(1)}, s32[3,4]{1,0:T(4,128)}, u32[]{:S(2)}) copy-start(s32[3,4]{1,0:T(4,128)} %index_ref.7) | copy-start | bytes 148
  0.0 7.5 %collective-permute-start.1 = (bf16[1,1024,512]{2,1,0:T(8,128)(2,1)}, bf16[1,1024,512]{2,1,0:T(8,128)(2,1)S(1)}, u32[]{:S(2)}, u32[]{:S(2)}) collective-permute-start(bf16[1,1024,512]{2,1,0:T(8,128)(2,1)} %in_a.3), channel_id=1, source_target_pairs={{0,1},{1,0},{2,3},{3,2},{4,5},{5,4},{6,7},{7,6},{8,9},{9,8},{10,11... | collective-permute-start | bytes 3145736 | tf_op jit(solution)/shard_map/ppermute | solution.py:231
  0.5 7.0 %collective-permute-start = (bf16[1,512,512]{2,1,0:T(8,128)(2,1)}, bf16[1,512,512]{2,1,0:T(8,128)(2,1)S(1)}, u32[]{:S(2)}, u32[]{:S(2)}) collective-permute-start(bf16[1,512,512]{2,1,0:T(8,128)(2,1)} %msg_a.3), channel_id=1, source_target_pairs={{0,1},{1,0},{2,3},{3,2},{4,5},{5,4},{6,7},{7,6},{8,9},{9,8},{10,11... | collective-permute-start | bytes 1572872 | tf_op jit(solution)/shard_map/ppermute | solution.py:231
  0.6 6.9 %collective-permute-start.2 = (bf16[1,512,512]{2,1,0:T(8,128)(2,1)}, bf16[1,512,512]{2,1,0:T(8,128)(2,1)S(1)}, u32[]{:S(2)}, u32[]{:S(2)}) collective-permute-start(bf16[1,512,512]{2,1,0:T(8,128)(2,1)} %out_a.3), channel_id=1, source_target_pairs={{0,1},{1,0},{2,3},{3,2},{4,5},{5,4},{6,7},{7,6},{8,9},{9,8},{10,11... | collective-permute-start | bytes 1572872 | tf_op jit(solution)/shard_map/ppermute | solution.py:231
  2.8 3.1 %collective-permute-start.3 = (f32[1,1024]{1,0:T(1,128)S(1)}, f32[1,1024]{1,0:T(1,128)S(1)}, u32[]{:S(2)}, u32[]{:S(2)}) collective-permute-start(f32[1,1024]{1,0:T(1,128)S(1)} %get-tuple-element.25.vec_a), channel_id=1, source_target_pairs={{0,1},{1,0},{2,3},{3,2},{4,5},{5,4},{6,7},{7,6},{8,9},{9,8},{10,11... | collective-permute-start | bytes 12296 | tf_op jit(solution)/shard_map/ppermute | solution.py:246
  3.0 9.5 %collective-permute-start.4 = (bf16[2,128,512]{2,1,0:T(8,128)(2,1)S(1)}, bf16[2,128,512]{2,1,0:T(8,128)(2,1)S(1)}, u32[]{:S(2)}, u32[]{:S(2)}) collective-permute-start(bf16[2,128,512]{2,1,0:T(8,128)(2,1)S(1)} %get-tuple-element.31), channel_id=1, source_target_pairs={{0,2},{1,3},{2,0},{3,1},{4,6},{5,7},{6,4},{7,5},{8,10},{9,11},{10,... | collective-permute-start | bytes 786440 | tf_op jit(solution)/shard_map/ppermute | solution.py:33
  5.9 8.2 %collective-permute-start.5 = (bf16[2,128,512]{2,1,0:T(8,128)(2,1)S(1)}, bf16[2,128,512]{2,1,0:T(8,128)(2,1)S(1)}, u32[]{:S(2)}, u32[]{:S(2)}) collective-permute-start(bf16[2,128,512]{2,1,0:T(8,128)(2,1)S(1)} %get-tuple-element.32), channel_id=1, source_target_pairs={{0,4},{1,5},{4,0},{5,1},{8,12},{9,13},{12,8},{13,9},{2,6},{3,7},{6... | collective-permute-start | bytes 786440 | tf_op jit(solution)/shard_map/ppermute | solution.py:33
  7.4 6.6 %collective-permute-start.6 = (bf16[2,128,512]{2,1,0:T(8,128)(2,1)S(1)}, bf16[2,128,512]{2,1,0:T(8,128)(2,1)S(1)}, u32[]{:S(2)}, u32[]{:S(2)}) collective-permute-start(bf16[2,128,512]{2,1,0:T(8,128)(2,1)S(1)} %get-tuple-element.33), channel_id=1, source_target_pairs={{0,1},{1,0},{4,8},{5,9},{8,4},{9,5},{12,13},{13,12},{2,3},{3,2},{6... | collective-permute-start | bytes 786440 | tf_op jit(solution)/shard_map/ppermute | solution.py:33
  7.5 6.6 %copy-start.2 = (s32[1,4,128]{2,1,0:T(4,128)S(1)}, s32[1,4,128]{2,1,0:T(4,128)}, u32[]{:S(2)}) copy-start(s32[1,4,128]{2,1,0:T(4,128)} %halo_ref.3) | copy-start | bytes 6148
  16.7 7.5 %collective-permute-start.7 = (bf16[2,128,512]{2,1,0:T(8,128)(2,1)S(1)}, bf16[2,128,512]{2,1,0:T(8,128)(2,1)S(1)}, u32[]{:S(2)}, u32[]{:S(2)}) collective-permute-start(bf16[2,128,512]{2,1,0:T(8,128)(2,1)S(1)} %get-tuple-element.40), channel_id=1, source_target_pairs={{0,2},{1,3},{2,0},{3,1},{4,6},{5,7},{6,4},{7,5},{8,10},{9,11},{10,... | collective-permute-start | bytes 786440 | tf_op jit(solution)/shard_map/ppermute | solution.py:33
  18.4 8.2 %collective-permute-start.8 = (bf16[2,128,512]{2,1,0:T(8,128)(2,1)S(1)}, bf16[2,128,512]{2,1,0:T(8,128)(2,1)S(1)}, u32[]{:S(2)}, u32[]{:S(2)}) collective-permute-start(bf16[2,128,512]{2,1,0:T(8,128)(2,1)S(1)} %get-tuple-element.41), channel_id=1, source_target_pairs={{0,4},{1,5},{4,0},{5,1},{8,12},{9,13},{12,8},{13,9},{2,6},{3,7},{6... | collective-permute-start | bytes 786440 | tf_op jit(solution)/shard_map/ppermute | solution.py:33
  21.1 5.5 %collective-permute-start.9 = (bf16[2,128,512]{2,1,0:T(8,128)(2,1)S(1)}, bf16[2,128,512]{2,1,0:T(8,128)(2,1)S(1)}, u32[]{:S(2)}, u32[]{:S(2)}) collective-permute-start(bf16[2,128,512]{2,1,0:T(8,128)(2,1)S(1)} %get-tuple-element.42), channel_id=1, source_target_pairs={{0,1},{1,0},{4,8},{5,9},{8,4},{9,5},{12,13},{13,12},{2,3},{3,2},{6... | collective-permute-start | bytes 786440 | tf_op jit(solution)/shard_map/ppermute | solution.py:33
